TPU v7x, 256 devices: a whole 4x4x8 slice. The times are simulated.
256 devices in a mesh: seq: 128 (over y, x, z), head: 2 (over core).
Axes of the slice: x: 4, y: 4, z: 8, core: 2. Of those that a mesh axis runs over, the one named last changes fastest.
Arguments:
- query_rows: bfloat16 [49152, 2048], P('seq', 'head'), may hold values from -41 to 41
- key_rows: bfloat16 [49152, 2048], P('seq', 'head'), may hold values from -4 to 4, as said below
- value_rows: bfloat16 [49152, 2048], P('seq', 'head'), may hold values from -6 to 6
- out_grad: bfloat16 [49152, 2048], P('seq'), may hold values from -6 to 6
- cluster_ids: int32 [16, 49152, 1], P('head', 'seq'), may hold values from 0 to 255; in each aligned block of 384 rows (0 to 383, 384 to 767, ..., all dimensions but the last counted through in order) at most 2 rows name the same one
- out_weight: bfloat16 [2048, 2048], P('head'), may hold values from -0.125 to 0.125
Outputs:
- layer_out: bfloat16 [49152, 2048], P('seq', 'head')
- query_grad: bfloat16 [49152, 2048], P('seq', 'head')
- key_grad: bfloat16 [49152, 2048], P('seq', 'head')
- value_grad: bfloat16 [49152, 2048], P('seq', 'head')
Inputs may be any that keep to these rules, and one draw needn't show every extreme that they name: `cluster_ids`: in each head the 384 tokens of one index of seq (aligned blocks of the token dimension) name no cluster more than 2 times, a bound that some block reaches in every draw. `key_rows`: no token's key in any head is all zeros.
All inputs are finite; a program needn't handle non-finite values.
Results may differ from a plain program's by a relative error of at most 0.009.
Values may be sent and summed in bfloat16 or wider, within the bound.
No kernel may reach another device: no remote copies, remote signals or barrier semaphores. Data moves between devices by JAX's collectives and lax.ppermute only.
A program may use at most 128 MiB of HBM per device.

v0:
```python
import jax
import jax.numpy as jnp
from jax import lax
from jax.sharding import PartitionSpec as P

CLUSTERS = 256
MOST = 2


NEGATIVE = -1e30


def slot_rows(cluster, per_cluster):
    count = cluster.shape[1]
    matches = cluster[:, :, None] == cluster[:, None, :]
    order_ids = jnp.arange(count, dtype=jnp.int32)
    earlier = order_ids[:, None] > order_ids[None, :]
    before = jnp.sum(jnp.logical_and(matches, earlier[None]).astype(jnp.int32), axis=2)
    return cluster * per_cluster + before


def fill_one(table, index_one, rows_one):
    return table.at[index_one].set(rows_one)


def take_one(table, index_one):
    return table[index_one]


def slot_marks(key_slots):
    return (jnp.max(jnp.abs(key_slots), axis=-1) > 0).astype(jnp.float32)


def forward_part(query_slots, key_slots, value_slots, occupied):
    scale = query_slots.shape[-1] ** (-0.5)
    scores = (
        jnp.einsum("hcqd,hckd->hcqk", query_slots, key_slots, preferred_element_type=jnp.float32)
        * scale
    )
    order_ids = jnp.arange(query_slots.shape[2], dtype=jnp.int32)
    causal = order_ids[None, :] <= order_ids[:, None]
    allowed = jnp.logical_and(causal[None, None], occupied[:, :, None, :] > 0)
    scores = jnp.where(allowed, scores, NEGATIVE)
    row_max = jnp.max(scores, axis=3, keepdims=True)
    weights = jnp.exp(scores - row_max)
    probs_full = weights / jnp.sum(weights, axis=3, keepdims=True)
    probs_half = probs_full.astype(jnp.bfloat16)
    attn_out = jnp.einsum(
        "hcqk,hckd->hcqd", probs_half, value_slots, preferred_element_type=jnp.float32
    ).astype(jnp.bfloat16)
    return (probs_full, probs_half, attn_out)


def backward_part(query_slots, key_slots, value_slots, grad_slots, probs_full, probs_half):
    scale = query_slots.shape[-1] ** (-0.5)
    dprob = jnp.einsum(
        "hcqd,hckd->hcqk", grad_slots, value_slots, preferred_element_type=jnp.float32
    )
    delta = jnp.sum(probs_full * dprob, axis=3, keepdims=True)
    dscore = (probs_full * (dprob - delta)).astype(jnp.bfloat16)
    query_part = (
        jnp.einsum("hcqk,hckd->hcqd", dscore, key_slots, preferred_element_type=jnp.float32) * scale
    ).astype(jnp.bfloat16)
    key_part = (
        jnp.einsum("hcqk,hcqd->hckd", dscore, query_slots, preferred_element_type=jnp.float32)
        * scale
    ).astype(jnp.bfloat16)
    value_part = jnp.einsum(
        "hcqk,hcqd->hckd", probs_half, grad_slots, preferred_element_type=jnp.float32
    ).astype(jnp.bfloat16)
    return (query_part, key_part, value_part)


def forward_work(received):
    query_slots = received[:, 0]
    key_slots = received[:, 1]
    value_slots = received[:, 2]
    probs_full, probs_half, attn_out = forward_part(
        query_slots, key_slots, value_slots, slot_marks(key_slots)
    )
    return jnp.stack([attn_out, query_slots, key_slots, value_slots], axis=1)


def body(query_rows, key_rows, value_rows, out_grad, cluster_ids, out_weight):
    tokens_here = query_rows.shape[0]
    heads_here = cluster_ids.shape[0]
    head_size = query_rows.shape[1] // heads_here
    slot_index = slot_rows(cluster_ids[:, :, 0], MOST)

    def to_slots(whole):
        split_rows = jnp.transpose(whole.reshape(tokens_here, heads_here, head_size), (1, 0, 2))
        empty = jnp.zeros((heads_here, CLUSTERS * MOST, head_size), whole.dtype)
        filled = jax.vmap(fill_one)(empty, slot_index, split_rows)
        return filled.reshape(heads_here, CLUSTERS, MOST, head_size)

    def to_tokens(slotted):
        table = slotted.reshape(heads_here, CLUSTERS * MOST, head_size)
        picked = jax.vmap(take_one)(table, slot_index)
        return jnp.transpose(picked, (1, 0, 2)).reshape(tokens_here, heads_here * head_size)

    attn_grad = jnp.dot(out_grad, out_weight.T, preferred_element_type=jnp.float32).astype(
        jnp.bfloat16
    )
    query_send = to_slots(query_rows)
    key_send = to_slots(key_rows)
    value_send = to_slots(value_rows)
    grad_send = to_slots(attn_grad)
    forward_send = jnp.stack([query_send, key_send, value_send], axis=1)
    owner_stack = forward_work(
        lax.all_to_all(forward_send, "seq", split_axis=2, concat_axis=3, tiled=True)
    )
    attn_back = lax.all_to_all(owner_stack[:, 0], "seq", split_axis=2, concat_axis=1, tiled=True)
    grad_owner = lax.all_to_all(grad_send, "seq", split_axis=1, concat_axis=2, tiled=True)
    query_owner = owner_stack[:, 1]
    key_owner = owner_stack[:, 2]
    value_owner = owner_stack[:, 3]
    probs_full, probs_half, attn_again = forward_part(
        query_owner, key_owner, value_owner, slot_marks(key_owner)
    )
    query_part, key_part, value_part = backward_part(
        query_owner, key_owner, value_owner, grad_owner, probs_full, probs_half
    )
    grads_back = lax.all_to_all(
        jnp.stack([query_part, key_part, value_part], axis=1),
        "seq",
        split_axis=3,
        concat_axis=2,
        tiled=True,
    )
    query_back = grads_back[:, 0]
    key_back = grads_back[:, 1]
    value_back = grads_back[:, 2]
    attn_local = to_tokens(attn_back)
    partial_out = jnp.dot(attn_local, out_weight, preferred_element_type=jnp.float32)
    layer_out = lax.psum_scatter(
        partial_out.astype(jnp.bfloat16), "head", scatter_dimension=1, tiled=True
    )
    return (layer_out, to_tokens(query_back), to_tokens(key_back), to_tokens(value_back))


def solution(mesh):
    in_specs = (
        P("seq", "head"),
        P("seq", "head"),
        P("seq", "head"),
        P("seq", None),
        P("head", "seq", None),
        P("head", None),
    )
    out_specs = (P("seq", "head"), P("seq", "head"), P("seq", "head"), P("seq", "head"))
    return jax.shard_map(body, mesh=mesh, in_specs=in_specs, out_specs=out_specs, check_vma=False)
```

profile of v0, /device:TPU:32, one launch (start us, length us, event | category | flops | bytes accessed | tf_op | source)
XLA Modules:
  0.0 398.4 jit_solution(535072671303252081)
XLA Ops:
  8.1 1.6 convert_reduce_fusion
  11.9 4.0 %fusion.9 = bf16[48,8,8,128]{3,2,1,0:T(8,128)(2,1)S(1)} fusion(bf16[384,2048]{1,0:T(8,128)(2,1)S(1)} %copy-done, bf16[1024,2048]{1,0:T(8,128)(2,1)} %param.11), kind=kOutput, calls=%fused_computation.31 | convolution fusion | flops 1611005952 | bytes 6553600 | tf_op jit(solution)/shard_map/dot_general | solution.py:101
  16.1 8.6 %scatter_custom_fusion.3 = bf16[4096,128]{1,0:T(8,128)(2,1)S(1)} fusion(s32[3072]{0:T(1024)S(1)} %reshape.128, bf16[3072,128]{1,0:T(8,128)(2,1)S(1)} %bitcast.135, bf16[]{:T(256)} %constant.9.clone.1), kind=kCustom, calls=%fused_computation.45 | custom fusion | bytes 1048578
  24.7 1.7 copy.119
  26.4 15.6 %all-to-all-start.2 = ((bf16[8,256,2,128]{3,2,0,1:T(2,128)(2,1)}), bf16[8,256,2,128]{3,2,0,1:T(2,128)(2,1)}, u32[]{:S(2)}, u32[]{:S(2)}) async-start(bf16[8,256,2,128]{3,2,0,1:T(2,128)(2,1)} %copy.119), calls=%async_computation.3 | async-start | bytes 2097152 | tf_op jit(solution)/shard_map/all_to_all | solution.py:113
  42.7 8.8 %scatter_custom_fusion.2 = bf16[4096,128]{1,0:T(8,128)(2,1)S(1)} fusion(s32[3072]{0:T(1024)S(1)} %reshape.128, bf16[3072,128]{1,0:T(8,128)(2,1)S(1)} %bitcast.136, bf16[]{:T(256)} %constant.9.clone.1), kind=kCustom, calls=%fused_computation.47 | custom fusion | bytes 1048578
  52.3 8.6 %scatter_custom_fusion = bf16[4096,128]{1,0:T(8,128)(2,1)S(1)} fusion(s32[3072]{0:T(1024)S(1)} %reshape.128, bf16[3072,128]{1,0:T(8,128)(2,1)S(1)} %bitcast.137, bf16[]{:T(256)} %constant.9.clone.1), kind=kCustom, calls=%fused_computation.51 | custom fusion | bytes 1048578
  63.5 8.9 %scatter_custom_fusion.1 = bf16[4096,128]{1,0:T(8,128)(2,1)S(1)} fusion(s32[3072]{0:T(1024)S(1)} %reshape.128, bf16[3072,128]{1,0:T(8,128)(2,1)} %bitcast.134, bf16[]{:T(256)} %constant.9.clone.1), kind=kCustom, calls=%fused_computation.49 | custom fusion | bytes 1049088
  72.5 5.3 %pad_maximum_fusion = bf16[8,3,256,2,128]{4,3,2,0,1:T(2,128)(2,1)S(1)} fusion(bf16[8,1,256,2,128]{4,3,2,0,1:T(2,128)(2,1)S(1)} %bitcast.121, bf16[8,1,256,2,128]{4,3,2,0,1:T(2,128)(2,1)S(1)} %bitcast.123, bf16[8,1,256,2,128]{4,3,2,0,1:T(2,128)(2,1)S(1)} %bitcast.122), kind=kLoop, calls=%fused_computation.14 | loop fusion | flops 3145728 | bytes 6291456 | tf_op jit(solution)/shard_map/stack | solution.py:108
  77.8 3.8 copy.111
  81.6 14.1 %all-to-all-start = ((bf16[8,3,256,2,128]{4,3,0,1,2:T(2,128)(2,1)}), bf16[8,3,256,2,128]{4,3,0,1,2:T(2,128)(2,1)S(1)}, u32[]{:S(2)}, u32[]{:S(2)}) async-start(bf16[8,3,256,2,128]{4,3,0,1,2:T(2,128)(2,1)} %copy.111), calls=%async_computation | async-start | bytes 6291456 | tf_op jit(solution)/shard_map/all_to_all | solution.py:110
  97.2 1.9 copy.121
  99.1 72.3 %all-to-all-done = bf16[8,3,256,2,128]{4,3,0,1,2:T(2,128)(2,1)S(1)} async-done(((bf16[8,3,256,2,128]{4,3,0,1,2:T(2,128)(2,1)}), bf16[8,3,256,2,128]{4,3,0,1,2:T(2,128)(2,1)S(1)}, u32[]{:S(2)}, u32[]{:S(2)}) %all-to-all-start) | async-done | bytes 3145760 | tf_op jit(solution)/shard_map/all_to_all | solution.py:110
  171.8 3.4 copy.113
  176.3 2.2 fusion.26
  180.6 2.7 multiply_reduce_fusion
  183.3 2.1 copy.115
  185.3 8.3 %all-to-all-start.1 = ((bf16[8,2,256,128]{3,1,0,2:T(2,128)(2,1)}), bf16[8,2,256,128]{3,1,0,2:T(2,128)(2,1)}, u32[]{:S(2)}, u32[]{:S(2)}) async-start(bf16[8,2,256,128]{3,1,0,2:T(2,128)(2,1)} %copy.115), calls=%async_computation.1 | async-start | bytes 2097152 | tf_op jit(solution)/shard_map/all_to_all | solution.py:112
  193.7 4.3 %multiply_convert_fusion = bf16[8,2,256,256]{2,3,1,0:T(8,128)(2,1)S(1)} fusion(f32[8,2,256,256]{2,3,1,0:T(8,128)} %get-tuple-element.12, f32[8,2,256]{2,1,0:T(2,128)S(1)} %get-tuple-element.11, f32[8,2,256,256]{2,3,1,0:T(8,128)} %copy-done.2, f32[8,2,256]{2,1,0:T(2,128)S(1)} %get-tuple-element.9), kind=kLoop, calls=%fused_computation.10 | loop fusion | flops 4194304 | bytes 10518528 | tf_op jit(solution)/shard_map/convert_element_type | solution.py:60
  202.1 4.9 %copy.123 = bf16[8,3,2,256,128]{4,2,0,1,3:T(2,128)(2,1)} copy(bf16[8,3,2,256,128]{4,3,2,0,1:T(8,128)(2,1)S(1)} %pad_maximum_fusion.1) | data formatting | bytes 6291456 | tf_op jit(solution)/shard_map/stack | solution.py:124
  207.0 15.5 %all-to-all-done.1 = bf16[8,2,256,128]{3,1,0,2:T(2,128)(2,1)} async-done(((bf16[8,2,256,128]{3,1,0,2:T(2,128)(2,1)}), bf16[8,2,256,128]{3,1,0,2:T(2,128)(2,1)}, u32[]{:S(2)}, u32[]{:S(2)}) %all-to-all-start.1) | async-done | bytes 1048608 | tf_op jit(solution)/shard_map/all_to_all | solution.py:112
  222.5 7.7 %all-to-all-start.3 = ((bf16[8,3,2,256,128]{4,2,0,1,3:T(2,128)(2,1)}), bf16[8,3,2,256,128]{4,2,0,1,3:T(2,128)(2,1)}, u32[]{:S(2)}, u32[]{:S(2)}) async-start(bf16[8,3,2,256,128]{4,2,0,1,3:T(2,128)(2,1)} %copy.123), calls=%async_computation.4 | async-start | bytes 6291456 | tf_op jit(solution)/shard_map/all_to_all | solution.py:123
  230.4 2.3 copy.116
  232.8 16.4 %gather_fusion = bf16[3072,128]{1,0:T(8,128)(2,1)S(1)} fusion(bf16[8,512,128]{2,1,0:T(8,128)(2,1)S(1)} %bitcast.107, s32[3072]{0:T(1024)S(1)} %reshape.104), kind=kCustom, calls=%fused_computation | custom fusion | bytes 1597440 | tf_op jit(solution)/shard_map/vmap()/gather | solution.py:27
  249.6 5.2 %convolution_convert_fusion = bf16[384,2048]{1,0:T(8,128)(2,1)} fusion(bf16[384,1024]{0,1:T(8,128)(2,1)S(1)} %bitcast.138, bf16[1024,2048]{1,0:T(8,128)(2,1)} %param.11), kind=kOutput, calls=%fused_computation.16 | convolution fusion | flops 1611399168 | bytes 6553600 | tf_op jit(solution)/shard_map/dot_general | solution.py:134
  254.7 47.7 %all-to-all-done.3 = bf16[8,3,2,256,128]{4,2,0,1,3:T(2,128)(2,1)} async-done(((bf16[8,3,2,256,128]{4,2,0,1,3:T(2,128)(2,1)}), bf16[8,3,2,256,128]{4,2,0,1,3:T(2,128)(2,1)}, u32[]{:S(2)}, u32[]{:S(2)}) %all-to-all-start.3) | async-done | bytes 3145760 | tf_op jit(solution)/shard_map/all_to_all | solution.py:123
  302.5 2.3 copy.124
  307.7 30.3 %gather_fusion.2 = bf16[3072,128]{1,0:T(8,128)(2,1)} fusion(bf16[8,512,128]{2,1,0:T(8,128)(2,1)S(1)} %bitcast.108, s32[3072]{0:T(1024)S(1)} %reshape.104), kind=kCustom, calls=%fused_computation.2 | custom fusion | bytes 1597440 | tf_op jit(solution)/shard_map/vmap()/gather | solution.py:27
  338.7 30.3 %gather_fusion.3 = bf16[3072,128]{1,0:T(8,128)(2,1)} fusion(bf16[8,512,128]{2,1,0:T(8,128)(2,1)S(1)} %bitcast.109, s32[3072]{0:T(1024)S(1)} %reshape.104), kind=kCustom, calls=%fused_computation.3 | custom fusion | bytes 1597440 | tf_op jit(solution)/shard_map/vmap()/gather | solution.py:27
  369.0 2.0 copy.126
  371.0 16.4 %gather_fusion.1 = bf16[3072,128]{1,0:T(8,128)(2,1)S(1)} fusion(bf16[8,512,128]{2,1,0:T(8,128)(2,1)S(1)} %bitcast.106, s32[3072]{0:T(1024)S(1)} %reshape.104), kind=kCustom, calls=%fused_computation.1 | custom fusion | bytes 1597440 | tf_op jit(solution)/shard_map/vmap()/gather | solution.py:27
  388.6 2.7 copy_bitcast_fusion
  (53 shorter events, 21.7 us)
Async XLA Ops:
  7.2 4.7 %copy-start = (bf16[384,2048]{1,0:T(8,128)(2,1)S(1)}, bf16[384,2048]{1,0:T(8,128)(2,1)}, u32[]{:S(2)}) copy-start(bf16[384,2048]{1,0:T(8,128)(2,1)} %param.9) | copy-start | bytes 4718596
  15.9 26.1 %copy-start.6 = (bf16[384,1024]{1,0:T(8,128)(2,1)S(1)}, bf16[384,1024]{1,0:T(8,128)(2,1)}, u32[]{:S(2)}) copy-start(bf16[384,1024]{1,0:T(8,128)(2,1)} %param.8) | copy-start | bytes 2359300
  26.4 25.1 %copy-start.7 = (bf16[384,1024]{1,0:T(8,128)(2,1)S(1)}, bf16[384,1024]{1,0:T(8,128)(2,1)}, u32[]{:S(2)}) copy-start(bf16[384,1024]{1,0:T(8,128)(2,1)} %param.6) | copy-start | bytes 2359300
  26.4 55.3 %all-to-all-start.2 = ((bf16[8,256,2,128]{3,2,0,1:T(2,128)(2,1)}), bf16[8,256,2,128]{3,2,0,1:T(2,128)(2,1)}, u32[]{:S(2)}, u32[]{:S(2)}) async-start(bf16[8,256,2,128]{3,2,0,1:T(2,128)(2,1)} %copy.119), calls=%async_computation.3 | async-start | bytes 2097152 | tf_op jit(solution)/shard_map/all_to_all | solution.py:113
  81.6 89.8 %all-to-all-start = ((bf16[8,3,256,2,128]{4,3,0,1,2:T(2,128)(2,1)}), bf16[8,3,256,2,128]{4,3,0,1,2:T(2,128)(2,1)S(1)}, u32[]{:S(2)}, u32[]{:S(2)}) async-start(bf16[8,3,256,2,128]{4,3,0,1,2:T(2,128)(2,1)} %copy.111), calls=%async_computation | async-start | bytes 6291456 | tf_op jit(solution)/shard_map/all_to_all | solution.py:110
  178.6 4.7 %copy-start.2 = (f32[8,2,256,256]{2,3,1,0:T(8,128)}, f32[8,2,256,256]{2,3,1,0:T(8,128)S(1)}, u32[]{:S(2)}) copy-start(f32[8,2,256,256]{2,3,1,0:T(8,128)S(1)} %get-tuple-element.10) | copy-start | bytes 12582916
  178.6 2.0 copy-start.4
  185.3 37.2 %all-to-all-start.1 = ((bf16[8,2,256,128]{3,1,0,2:T(2,128)(2,1)}), bf16[8,2,256,128]{3,1,0,2:T(2,128)(2,1)}, u32[]{:S(2)}, u32[]{:S(2)}) async-start(bf16[8,2,256,128]{3,1,0,2:T(2,128)(2,1)} %copy.115), calls=%async_computation.1 | async-start | bytes 2097152 | tf_op jit(solution)/shard_map/all_to_all | solution.py:112
  197.9 1.5 copy-start.5
  198.7 2.3 copy-start.3
  222.5 80.0 %all-to-all-start.3 = ((bf16[8,3,2,256,128]{4,2,0,1,3:T(2,128)(2,1)}), bf16[8,3,2,256,128]{4,2,0,1,3:T(2,128)(2,1)}, u32[]{:S(2)}, u32[]{:S(2)}) async-start(bf16[8,3,2,256,128]{4,2,0,1,3:T(2,128)(2,1)} %copy.123), calls=%async_computation.4 | async-start | bytes 6291456 | tf_op jit(solution)/shard_map/all_to_all | solution.py:123
  230.2 161.1 %reduce-scatter.2.cloned.1.call-start = ((), (), s32[]{:S(2)}) async-start(), calls=%async_computation.5 | async-start | bytes 2359296 | tf_op jit(solution)/shard_map/reduce_scatter | solution.py:135
  371.0 20.3 %copy-start.1 = (bf16[384,2048]{1,0:T(8,128)(2,1)S(1)}, bf16[384,2048]{1,0:T(8,128)(2,1)}, u32[]{:S(2)}) copy-start(bf16[384,2048]{1,0:T(8,128)(2,1)} %param.9) | copy-start | bytes 4718596
Sparse Core Ops, SparseCore 0:
  254.9 15.9 reduce-scatter.1
where the time goes:
time: 406 us; the launch traced here: 398 us
  local copies, waits for them, and re-layouts  170 us (42%)
  waiting for transfers between devices  136 us (33%)
  starting transfers between devices  45.9 us (11%)
  other arithmetic  16.5 us (4%)
  matrix products  15.6 us (4%)
  between operations  14.6 us (4%)
    gather x5, local copies, waits for them, and re-layouts, take_one(): return table[index_one]  93.7 us
    all_to_all x1, waiting for transfers between devices, body(): lax.all_to_all(forward_send, 'seq', split_axis=2, concat_axis=3, tiled=True)  72.3 us
    all_to_all x1, waiting for transfers between devices, body(): lax.all_to_all(jnp.stack([query_part, key_part, value_part], axis=1), 'se...  47.7 us
    unnamed x25, local copies, waits for them, and re-layouts  40.6 us
    all_to_all x1, starting transfers between devices, body(): lax.all_to_all(grad_send, 'seq', split_axis=1, concat_axis=2, tiled=True)  15.6 us
    all_to_all x1, waiting for transfers between devices, body(): lax.all_to_all(owner_stack[:, 0], 'seq', split_axis=2, concat_axis=1, til...  15.5 us
    all_to_all x1, starting transfers between devices, body(): lax.all_to_all(forward_send, 'seq', split_axis=2, concat_axis=3, tiled=True)  14.1 us
    all_to_all x1, starting transfers between devices, body(): lax.all_to_all(owner_stack[:, 0], 'seq', split_axis=2, concat_axis=1, til...  8.29 us
  transfers between devices with their start and end apart: 5, of which 3 were waited for; matrix products, arithmetic and copies ran while one was open for 42% of the time, Pallas kernels for 0%

commit v1 on v0

v1 whole, which is shorter than its diff:
```python
import functools

import jax
import jax.numpy as jnp
from jax import lax
from jax.experimental import pallas as pl
from jax.experimental.pallas import tpu as pltpu
from jax.sharding import PartitionSpec as P

CLUSTERS = 256
MOST = 2
DH = 128
SEQ = 128
HEADS = 8
TOK = 384
PER_HEAD = CLUSTERS * MOST
OWNERS = SEQ // HEADS
ROWS = PER_HEAD // OWNERS
OWNED = ROWS // MOST
SLOTS = SEQ * MOST
GROUP = 8
EMPTY = 64.0
NEGATIVE = -1e30
SCALE = DH ** -0.5
F32 = jnp.float32
BF16 = jnp.bfloat16


def slot_of_row(ids_row, ids_col):
    u = lax.broadcasted_iota(jnp.int32, (TOK, TOK), 0)
    t = lax.broadcasted_iota(jnp.int32, (TOK, TOK), 1)
    same = jnp.logical_and(ids_col == ids_row, u < t)
    before = jnp.max(jnp.where(same, 1, 0), axis=0, keepdims=True)
    return ids_row * MOST + before


def slot_of_col(ids_row, ids_col):
    t = lax.broadcasted_iota(jnp.int32, (TOK, TOK), 0)
    u = lax.broadcasted_iota(jnp.int32, (TOK, TOK), 1)
    same = jnp.logical_and(ids_col == ids_row, u < t)
    before = jnp.max(jnp.where(same, 1, 0), axis=1, keepdims=True)
    return ids_col * MOST + before


def send_mask(idr_ref, idc_ref):
    slot = slot_of_row(idr_ref[0], idc_ref[0])
    rows = lax.broadcasted_iota(jnp.int32, (PER_HEAD, TOK), 0)
    return jnp.where(rows == slot, 1.0, 0.0).astype(BF16)


def take_mask(idr_ref, idc_ref):
    slot = slot_of_col(idr_ref[0], idc_ref[0])
    cols = lax.broadcasted_iota(jnp.int32, (TOK, PER_HEAD), 1)
    return jnp.where(cols == slot, 1.0, 0.0).astype(BF16)


def dispatch_qkv_kernel(idr_ref, idc_ref, q_ref, k_ref, v_ref, out_ref):
    mask = send_mask(idr_ref, idc_ref)
    whole = jnp.concatenate([q_ref[...], k_ref[...], v_ref[...], jnp.ones((TOK, DH), BF16)], axis=1)
    got = jnp.dot(mask, whole, preferred_element_type=F32)
    key = got[:, DH : 2 * DH] + EMPTY * (1.0 - got[:, 3 * DH :])
    out_ref[:, 0] = got[:, :DH].astype(BF16).reshape(OWNERS, ROWS, DH)
    out_ref[:, 1] = key.astype(BF16).reshape(OWNERS, ROWS, DH)
    out_ref[:, 2] = got[:, 2 * DH : 3 * DH].astype(BF16).reshape(OWNERS, ROWS, DH)


def dispatch_one_kernel(idr_ref, idc_ref, g_ref, out_ref):
    mask = send_mask(idr_ref, idc_ref)
    got = jnp.dot(mask, g_ref[...], preferred_element_type=F32)
    out_ref[...] = got.astype(BF16).reshape(OWNERS, ROWS, DH)


def combine_one_kernel(idr_ref, idc_ref, a_ref, out_ref):
    mask = take_mask(idr_ref, idc_ref)
    got = jnp.dot(mask, a_ref[...].reshape(PER_HEAD, DH), preferred_element_type=F32)
    out_ref[...] = got.astype(BF16)


def combine_grads_kernel(idr_ref, idc_ref, a_ref, dq_ref, dk_ref, dv_ref):
    mask = take_mask(idr_ref, idc_ref)
    whole = jnp.concatenate([a_ref[:, j].reshape(PER_HEAD, DH) for j in range(3)], axis=1)
    got = jnp.dot(mask, whole, preferred_element_type=F32).astype(BF16)
    dq_ref[...] = got[:, :DH]
    dk_ref[...] = got[:, DH : 2 * DH]
    dv_ref[...] = got[:, 2 * DH :]


def id_specs():
    return [
        pl.BlockSpec((1, 1, TOK), lambda h: (h, 0, 0)),
        pl.BlockSpec((1, TOK, 1), lambda h: (h, 0, 0)),
    ]


def token_spec():
    return pl.BlockSpec((TOK, DH), lambda h: (0, h))


def dispatch_qkv(idr, idc, q, k, v):
    return pl.pallas_call(
        dispatch_qkv_kernel,
        grid=(HEADS,),
        in_specs=id_specs() + [token_spec()] * 3,
        out_specs=pl.BlockSpec((OWNERS, 3, ROWS, DH), lambda h: (h, 0, 0, 0)),
        out_shape=jax.ShapeDtypeStruct((SEQ, 3, ROWS, DH), BF16),
        name="dispatch_qkv",
    )(idr, idc, q, k, v)


def dispatch_one(idr, idc, g):
    return pl.pallas_call(
        dispatch_one_kernel,
        grid=(HEADS,),
        in_specs=id_specs() + [token_spec()],
        out_specs=pl.BlockSpec((OWNERS, ROWS, DH), lambda h: (h, 0, 0)),
        out_shape=jax.ShapeDtypeStruct((SEQ, ROWS, DH), BF16),
        name="dispatch_one",
    )(idr, idc, g)


def combine_one(idr, idc, a):
    return pl.pallas_call(
        combine_one_kernel,
        grid=(HEADS,),
        in_specs=id_specs() + [pl.BlockSpec((OWNERS, ROWS, DH), lambda h: (h, 0, 0))],
        out_specs=token_spec(),
        out_shape=jax.ShapeDtypeStruct((TOK, HEADS * DH), BF16),
        name="combine_one",
    )(idr, idc, a)


def combine_grads(idr, idc, a):
    return pl.pallas_call(
        combine_grads_kernel,
        grid=(HEADS,),
        in_specs=id_specs() + [pl.BlockSpec((OWNERS, 3, ROWS, DH), lambda h: (h, 0, 0, 0))],
        out_specs=[token_spec()] * 3,
        out_shape=[jax.ShapeDtypeStruct((TOK, HEADS * DH), BF16)] * 3,
        name="combine_grads",
    )(idr, idc, a)


PB = GROUP * ROWS


def regroup_matrix(inverse):
    a = lax.broadcasted_iota(jnp.int32, (PB, PB), 1 if inverse else 0)
    b = lax.broadcasted_iota(jnp.int32, (PB, PB), 0 if inverse else 1)
    per = GROUP * MOST
    want = ((a % per) // MOST) * ROWS + (a // per) * MOST + a % MOST
    return jnp.where(b == want, 1.0, 0.0).astype(BF16)


def matmul(a, b, dims):
    return lax.dot_general(a, b, (dims, ((), ())), preferred_element_type=F32)


NT = ((1,), (1,))
NN = ((1,), (0,))
TN = ((0,), (0,))


def probabilities(q, k):
    scores = matmul(q, k, NT) * SCALE
    pick = jnp.where(lax.broadcasted_iota(jnp.int32, (8, DH), 1) == 0, 1.0, 0.0).astype(BF16)
    first = matmul(pick, k, NT)[0:1, :]
    t = lax.broadcasted_iota(jnp.int32, (SLOTS, SLOTS), 0)
    u = lax.broadcasted_iota(jnp.int32, (SLOTS, SLOTS), 1)
    allowed = jnp.logical_and(u <= t, first < 0.5 * EMPTY)
    scores = jnp.where(allowed, scores, NEGATIVE)
    weights = jnp.exp(scores - jnp.max(scores, axis=1, keepdims=True))
    return weights / jnp.sum(weights, axis=1, keepdims=True)


def regroup_in(perm, pieces, targets):
    whole = jnp.concatenate(pieces, axis=1)
    got = jnp.dot(perm, whole, preferred_element_type=F32).astype(BF16)
    return [got[:, i * DH : (i + 1) * DH].reshape(OWNED, GROUP * MOST, DH) for i in range(len(pieces))]


def forward_kernel(in_ref, qs_ref, ks_ref, vs_ref, out_ref, attn_ref):
    perm = regroup_matrix(False)
    for g in range(SEQ // GROUP):
        src = slice(g * GROUP, (g + 1) * GROUP)
        dst = slice(g * GROUP * MOST, (g + 1) * GROUP * MOST)
        pieces = [in_ref[src, j].reshape(PB, DH) for j in range(3)]
        q, k, v = regroup_in(perm, pieces, None)
        qs_ref[:, dst, :] = q
        ks_ref[:, dst, :] = k
        vs_ref[:, dst, :] = v

    def one(c, carry):
        p = probabilities(qs_ref[c], ks_ref[c]).astype(BF16)
        attn_ref[c] = matmul(p, vs_ref[c], NN).astype(BF16)
        return carry

    lax.fori_loop(0, OWNED, one, 0)
    back = regroup_matrix(True)
    for g in range(SEQ // GROUP):
        src = slice(g * GROUP, (g + 1) * GROUP)
        dst = slice(g * GROUP * MOST, (g + 1) * GROUP * MOST)
        y = attn_ref[:, dst, :].reshape(PB, DH)
        out_ref[src] = jnp.dot(back, y, preferred_element_type=F32).astype(BF16).reshape(GROUP, ROWS, DH)


def backward_kernel(g_ref, qs_ref, ks_ref, vs_ref, out_ref, gs_ref, dq_ref, dk_ref, dv_ref):
    perm = regroup_matrix(False)
    for g in range(SEQ // GROUP):
        src = slice(g * GROUP, (g + 1) * GROUP)
        dst = slice(g * GROUP * MOST, (g + 1) * GROUP * MOST)
        (gg,) = regroup_in(perm, [g_ref[src].reshape(PB, DH)], None)
        gs_ref[:, dst, :] = gg

    def one(c, carry):
        q, k, v, g = qs_ref[c], ks_ref[c], vs_ref[c], gs_ref[c]
        p = probabilities(q, k)
        dp = matmul(g, v, NT)
        delta = jnp.sum(p * dp, axis=1, keepdims=True)
        ds = (p * (dp - delta)).astype(BF16)
        dq_ref[c] = (matmul(ds, k, NN) * SCALE).astype(BF16)
        dk_ref[c] = (matmul(ds, q, TN) * SCALE).astype(BF16)
        dv_ref[c] = matmul(p.astype(BF16), g, TN).astype(BF16)
        return carry

    lax.fori_loop(0, OWNED, one, 0)
    back = regroup_matrix(True)
    for g in range(SEQ // GROUP):
        src = slice(g * GROUP, (g + 1) * GROUP)
        dst = slice(g * GROUP * MOST, (g + 1) * GROUP * MOST)
        y = jnp.concatenate([r[:, dst, :].reshape(PB, DH) for r in (dq_ref, dk_ref, dv_ref)], axis=1)
        got = jnp.dot(back, y, preferred_element_type=F32).astype(BF16)
        for j in range(3):
            out_ref[src, j] = got[:, j * DH : (j + 1) * DH].reshape(GROUP, ROWS, DH)


VM = pl.BlockSpec(memory_space=pltpu.VMEM)
GROUPED = (OWNED, SLOTS, DH)


def forward(received):
    return pl.pallas_call(
        forward_kernel,
        in_specs=[VM],
        out_specs=[VM] * 4,
        out_shape=[jax.ShapeDtypeStruct(GROUPED, BF16)] * 3 + [jax.ShapeDtypeStruct((SEQ, ROWS, DH), BF16)],
        scratch_shapes=[pltpu.VMEM(GROUPED, BF16)],
        name="cluster_forward",
    )(received)


def backward(received, qs, ks, vs):
    return pl.pallas_call(
        backward_kernel,
        in_specs=[VM] * 4,
        out_specs=VM,
        out_shape=jax.ShapeDtypeStruct((SEQ, 3, ROWS, DH), BF16),
        scratch_shapes=[pltpu.VMEM(GROUPED, BF16)] * 4,
        name="cluster_backward",
    )(received, qs, ks, vs)


def exchange(x):
    return lax.all_to_all(x, "seq", split_axis=0, concat_axis=0, tiled=True)


def body(query_rows, key_rows, value_rows, out_grad, cluster_ids, out_weight):
    idr = jnp.transpose(cluster_ids, (0, 2, 1))
    idc = cluster_ids
    qkv = exchange(dispatch_qkv(idr, idc, query_rows, key_rows, value_rows))
    attn_grad = lax.dot_general(
        out_grad, out_weight, (((1,), (1,)), ((), ())), preferred_element_type=F32
    ).astype(BF16)
    g_slots = exchange(dispatch_one(idr, idc, attn_grad))
    qs, ks, vs, attn_slots = forward(qkv)
    attn_back = exchange(attn_slots)
    grads_back = exchange(backward(g_slots, qs, ks, vs))
    attn = combine_one(idr, idc, attn_back)
    partial_out = jnp.dot(attn, out_weight, preferred_element_type=F32)
    half = partial_out.shape[1] // 2
    core = lax.axis_index("head")
    low, high = partial_out[:, :half], partial_out[:, half:]
    mine = jnp.where(core == 0, low, high)
    other = jnp.where(core == 0, high, low).astype(BF16)
    came = lax.ppermute(other, "head", [(0, 1), (1, 0)])
    layer_out = (mine + came.astype(F32)).astype(BF16)
    dq, dk, dv = combine_grads(idr, idc, grads_back)
    return layer_out, dq, dk, dv


def solution(mesh):
    in_specs = (
        P("seq", "head"),
        P("seq", "head"),
        P("seq", "head"),
        P("seq", None),
        P("head", "seq", None),
        P("head", None),
    )
    out_specs = (P("seq", "head"), P("seq", "head"), P("seq", "head"), P("seq", "head"))
    return jax.shard_map(body, mesh=mesh, in_specs=in_specs, out_specs=out_specs, check_vma=False)
```

time: 406 us -> 264 us (0.65); the launches traced: 398 us -> 263 us
  local copies, waits for them, and re-layouts: 170 us -> 2.5 us
  Pallas kernels: 0 us -> 66.7 us
  other arithmetic: 16.5 us -> 1.47 us
  between operations: 14.6 us -> 0.72 us
  waiting for transfers between devices: 136 us -> 145 us
  starting transfers between devices: 45.9 us -> 37.5 us
  matrix products: 15.6 us -> 9.11 us
    gather x5 -> x0, local copies, waits for them, and re-layouts: 93.7 us -> none  [take_one(): return table[index_one]]
    pallas_call x0 -> x6, Pallas kernels: none -> 66.7 us  [the longest x1 17.5 us: backward(): pl.pallas_call(backward_kernel, in_specs=[VM] * 4, out_specs=VM, out_shap...]
    unnamed x25 -> x5, local copies, waits for them, and re-layouts: 40.6 us -> 2.5 us
    all_to_all x7 -> x0, local copies, waits for them, and re-layouts: 12.2 us -> none  [the longest x2 3.79 us: body(): lax.all_to_all(forward_send, 'seq', split_axis=2, concat_axis=3, tiled=True)]
    another operation x2 -> x0, local copies, waits for them, and re-layouts: 8.73 us -> none  [the longest x1 4.9 us: body(): jnp.stack([query_part, key_part, value_part], axis=1)]
    all_to_all x4, starting transfers between devices: 45.7 us -> 37.4 us  [exchange(): return lax.all_to_all(x, 'seq', split_axis=0, concat_axis=0, tiled=True)]
    all_to_all x4, waiting for transfers between devices: 136 us -> 143 us  [exchange(): return lax.all_to_all(x, 'seq', split_axis=0, concat_axis=0, tiled=True)]
    dot_general x8 -> x2, matrix products: 15.6 us -> 9.11 us  [the longest x1 4.89 us: body(): lax.dot_general(out_grad, out_weight, (((1,), (1,)), ((), ())), preferred...]
  transfers between devices with their start and end apart: 5 -> 5, of which waited for: 3 -> 5; matrix products, arithmetic and copies ran while one was open for 42% -> 4% of each run, Pallas kernels for 0% -> 18%
where the time goes in v1:
time: 264 us; the launch traced here: 263 us
  waiting for transfers between devices  145 us (55%)
  Pallas kernels  66.7 us (25%)
  starting transfers between devices  37.5 us (14%)
  matrix products  9.11 us (3%)
    all_to_all x4, waiting for transfers between devices, exchange(): return lax.all_to_all(x, 'seq', split_axis=0, concat_axis=0, tiled=True)  143 us
    all_to_all x4, starting transfers between devices, exchange(): return lax.all_to_all(x, 'seq', split_axis=0, concat_axis=0, tiled=True)  37.4 us
    pallas_call x1, Pallas kernels, backward(): pl.pallas_call(backward_kernel, in_specs=[VM] * 4, out_specs=VM, out_shap...  17.5 us
    pallas_call x1, Pallas kernels, forward(): pl.pallas_call(forward_kernel, in_specs=[VM], out_specs=[VM] * 4, out_sha...  14.6 us
    pallas_call x1, Pallas kernels, combine_grads(): pl.pallas_call(combine_grads_kernel, grid=(HEADS,), in_specs=id_specs() +...  10.1 us
    pallas_call x1, Pallas kernels, combine_one(): pl.pallas_call(combine_one_kernel, grid=(HEADS,), in_specs=id_specs() + [...  8.86 us
    pallas_call x1, Pallas kernels, dispatch_qkv(): pl.pallas_call(dispatch_qkv_kernel, grid=(HEADS,), in_specs=id_specs() +...  8.49 us
    pallas_call x1, Pallas kernels, dispatch_one(): pl.pallas_call(dispatch_one_kernel, grid=(HEADS,), in_specs=id_specs() +...  7.1 us
  transfers between devices with their start and end apart: 5, of which 5 were waited for; matrix products, arithmetic and copies ran while one was open for 4% of the time, Pallas kernels for 18%

profile of v1, /device:TPU:32, one launch (start us, length us, event | category | flops | bytes accessed | tf_op | source)
XLA Modules:
  0.0 263.0 jit_solution(16512466685180534384)
XLA Ops:
  0.6 0.0 copy-start
  0.6 2.5 copy.11.idc_ref
  3.1 8.5 %dispatch_qkv.1 = bf16[128,3,32,128]{3,2,1,0:T(8,128)(2,1)} custom-call(s32[8,1,384]{2,1,0:T(1,128)} %bitcast.5, s32[8,384,1]{2,1,0:T(8,128)} %copy.11.idc_ref, bf16[384,1024]{1,0:T(8,128)(2,1)} %q_ref.1, bf16[384,1024]{1,0:T(8,128)(2,1)} %k_ref.1, bf16[384,1024]{1,0:T(8,128)(2,1)} %v_ref.1), custom_call_target="tpu_custom_call" | custom-call | tf_op jit(solution)/shard_map/dispatch_qkv/pallas_call | solution.py:100
  11.6 15.4 %all-to-all-start = ((bf16[128,3,32,128]{3,2,1,0:T(8,128)(2,1)}), bf16[128,3,32,128]{3,2,1,0:T(8,128)(2,1)}, u32[]{:S(2)}, u32[]{:S(2)}) async-start(bf16[128,3,32,128]{3,2,1,0:T(8,128)(2,1)} %dispatch_qkv.1), calls=%async_computation | async-start | bytes 6291456 | tf_op jit(solution)/shard_map/all_to_all | solution.py:263
  27.0 0.0 copy-done
  27.0 4.9 %convolution_convert_fusion.g_ref = bf16[384,1024]{1,0:T(8,128)(2,1)} fusion(bf16[384,2048]{1,0:T(8,128)(2,1)S(1)} %copy-done, bf16[1024,2048]{1,0:T(8,128)(2,1)} %param.11), kind=kOutput, calls=%fused_computation.2 | convolution fusion | flops 1611005952 | bytes 6553600 | tf_op jit(solution)/shard_map/dot_general | solution.py:270
  31.9 7.1 %dispatch_one.1 = bf16[128,32,128]{2,1,0:T(8,128)(2,1)} custom-call(s32[8,1,384]{2,1,0:T(1,128)} %bitcast.6, s32[8,384,1]{2,1,0:T(8,128)} %copy.11.idc_ref, bf16[384,1024]{1,0:T(8,128)(2,1)} %convolution_convert_fusion.g_ref), custom_call_target="tpu_custom_call" | custom-call | tf_op jit(solution)/shard_map/dispatch_one/pallas_call | solution.py:111
  39.0 64.0 %all-to-all-done.in_ref = bf16[128,3,32,128]{3,2,1,0:T(8,128)(2,1)} async-done(((bf16[128,3,32,128]{3,2,1,0:T(8,128)(2,1)}), bf16[128,3,32,128]{3,2,1,0:T(8,128)(2,1)}, u32[]{:S(2)}, u32[]{:S(2)}) %all-to-all-start) | async-done | bytes 3145760 | tf_op jit(solution)/shard_map/all_to_all | solution.py:263
  103.0 6.6 %all-to-all-start.2 = ((bf16[128,32,128]{2,1,0:T(8,128)(2,1)}), bf16[128,32,128]{2,1,0:T(8,128)(2,1)S(1)}, u32[]{:S(2)}, u32[]{:S(2)}) async-start(bf16[128,32,128]{2,1,0:T(8,128)(2,1)} %dispatch_one.1), calls=%async_computation.2 | async-start | bytes 2097152 | tf_op jit(solution)/shard_map/all_to_all | solution.py:263
  109.7 14.6 %cluster_forward.1 = (bf16[16,256,128]{2,1,0:T(8,128)(2,1)}, bf16[16,256,128]{2,1,0:T(8,128)(2,1)}, bf16[16,256,128]{2,1,0:T(8,128)(2,1)}, bf16[128,32,128]{2,1,0:T(8,128)(2,1)}) custom-call(bf16[128,3,32,128]{3,2,1,0:T(8,128)(2,1)} %all-to-all-done.in_ref), custom_call_target="tpu_custom_call" | custom-call | tf_op jit(solution)/shard_map/cluster_forward/pallas_call | solution.py:241
  124.3 15.0 %all-to-all-done.2.g_ref = bf16[128,32,128]{2,1,0:T(8,128)(2,1)S(1)} async-done(((bf16[128,32,128]{2,1,0:T(8,128)(2,1)}), bf16[128,32,128]{2,1,0:T(8,128)(2,1)S(1)}, u32[]{:S(2)}, u32[]{:S(2)}) %all-to-all-start.2) | async-done | bytes 1048608 | tf_op jit(solution)/shard_map/all_to_all | solution.py:263
  139.3 0.0 copy-start.1
  139.3 7.7 %all-to-all-start.1 = ((bf16[128,32,128]{2,1,0:T(8,128)(2,1)}), bf16[128,32,128]{2,1,0:T(8,128)(2,1)}, u32[]{:S(2)}, u32[]{:S(2)}) async-start(bf16[128,32,128]{2,1,0:T(8,128)(2,1)} %get-tuple-element.11), calls=%async_computation.1 | async-start | bytes 2097152 | tf_op jit(solution)/shard_map/all_to_all | solution.py:263
  147.0 0.0 copy-done.1
  147.0 17.5 %cluster_backward.1 = bf16[128,3,32,128]{3,2,1,0:T(8,128)(2,1)} custom-call(bf16[128,32,128]{2,1,0:T(8,128)(2,1)} %copy-done.1, bf16[16,256,128]{2,1,0:T(8,128)(2,1)} %get-tuple-element.12.qs_ref, bf16[16,256,128]{2,1,0:T(8,128)(2,1)} %get-tuple-element.13.ks_ref, bf16[16,256,128]{2,1,0:T(8,128)(2,1)} %get-tuple-element.14.vs_ref), custom_call_target="tpu_custom_call" | custom-call | tf_op jit(solution)/shard_map/cluster_backward/pallas_call | solution.py:252
  164.5 9.9 %all-to-all-done.1.a_ref = bf16[128,32,128]{2,1,0:T(8,128)(2,1)} async-done(((bf16[128,32,128]{2,1,0:T(8,128)(2,1)}), bf16[128,32,128]{2,1,0:T(8,128)(2,1)}, u32[]{:S(2)}, u32[]{:S(2)}) %all-to-all-start.1) | async-done | bytes 1048608 | tf_op jit(solution)/shard_map/all_to_all | solution.py:263
  174.4 7.7 %all-to-all-start.3 = ((bf16[128,3,32,128]{3,2,1,0:T(8,128)(2,1)}), bf16[128,3,32,128]{3,2,1,0:T(8,128)(2,1)}, u32[]{:S(2)}, u32[]{:S(2)}) async-start(bf16[128,3,32,128]{3,2,1,0:T(8,128)(2,1)} %cluster_backward.1), calls=%async_computation.3 | async-start | bytes 6291456 | tf_op jit(solution)/shard_map/all_to_all | solution.py:263
  182.2 8.9 %combine_one.1 = bf16[384,1024]{1,0:T(8,128)(2,1)} custom-call(s32[8,1,384]{2,1,0:T(1,128)} %bitcast.7, s32[8,384,1]{2,1,0:T(8,128)} %copy.11.idc_ref, bf16[128,32,128]{2,1,0:T(8,128)(2,1)} %all-to-all-done.1.a_ref), custom_call_target="tpu_custom_call" | custom-call | tf_op jit(solution)/shard_map/combine_one/pallas_call | solution.py:122
  191.0 4.2 %fusion = f32[384,2048]{1,0:T(8,128)S(1)} fusion(bf16[384,1024]{1,0:T(8,128)(2,1)} %combine_one.1, bf16[1024,2048]{1,0:T(8,128)(2,1)} %param.11), kind=kOutput, calls=%fused_computation.3 | convolution fusion | flops 1610612736 | bytes 8126464 | tf_op jit(solution)/shard_map/dot_general | solution.py:278
  195.2 0.1 select_convert_fusion
  195.4 0.1 collective-permute-start
  195.5 2.3 collective-permute-done
  197.8 1.3 add_convert_fusion
  199.1 53.8 %all-to-all-done.3.a_ref = bf16[128,3,32,128]{3,2,1,0:T(8,128)(2,1)} async-done(((bf16[128,3,32,128]{3,2,1,0:T(8,128)(2,1)}), bf16[128,3,32,128]{3,2,1,0:T(8,128)(2,1)}, u32[]{:S(2)}, u32[]{:S(2)}) %all-to-all-start.3) | async-done | bytes 3145760 | tf_op jit(solution)/shard_map/all_to_all | solution.py:263
  252.9 10.1 %combine_grads.1 = (bf16[384,1024]{1,0:T(8,128)(2,1)}, bf16[384,1024]{1,0:T(8,128)(2,1)}, bf16[384,1024]{1,0:T(8,128)(2,1)}) custom-call(s32[8,1,384]{2,1,0:T(1,128)} %bitcast.8, s32[8,384,1]{2,1,0:T(8,128)} %copy.11.idc_ref, bf16[128,3,32,128]{3,2,1,0:T(8,128)(2,1)} %all-to-all-done.3.a_ref), custom_call_target="tpu_custom_call" | custom-call | tf_op jit(solution)/shard_map/combine_grads/pallas_call | solution.py:133
Async XLA Ops:
  0.6 26.4 %copy-start = (bf16[384,2048]{1,0:T(8,128)(2,1)S(1)}, bf16[384,2048]{1,0:T(8,128)(2,1)}, u32[]{:S(2)}) copy-start(bf16[384,2048]{1,0:T(8,128)(2,1)} %param.9) | copy-start | bytes 4718596
  11.6 91.4 %all-to-all-start = ((bf16[128,3,32,128]{3,2,1,0:T(8,128)(2,1)}), bf16[128,3,32,128]{3,2,1,0:T(8,128)(2,1)}, u32[]{:S(2)}, u32[]{:S(2)}) async-start(bf16[128,3,32,128]{3,2,1,0:T(8,128)(2,1)} %dispatch_qkv.1), calls=%async_computation | async-start | bytes 6291456 | tf_op jit(solution)/shard_map/all_to_all | solution.py:263
  103.0 36.2 %all-to-all-start.2 = ((bf16[128,32,128]{2,1,0:T(8,128)(2,1)}), bf16[128,32,128]{2,1,0:T(8,128)(2,1)S(1)}, u32[]{:S(2)}, u32[]{:S(2)}) async-start(bf16[128,32,128]{2,1,0:T(8,128)(2,1)} %dispatch_one.1), calls=%async_computation.2 | async-start | bytes 2097152 | tf_op jit(solution)/shard_map/all_to_all | solution.py:263
  139.3 7.7 %copy-start.1 = (bf16[128,32,128]{2,1,0:T(8,128)(2,1)}, bf16[128,32,128]{2,1,0:T(8,128)(2,1)S(1)}, u32[]{:S(2)}) copy-start(bf16[128,32,128]{2,1,0:T(8,128)(2,1)S(1)} %all-to-all-done.2.g_ref) | copy-start | bytes 3145732
  139.3 35.2 %all-to-all-start.1 = ((bf16[128,32,128]{2,1,0:T(8,128)(2,1)}), bf16[128,32,128]{2,1,0:T(8,128)(2,1)}, u32[]{:S(2)}, u32[]{:S(2)}) async-start(bf16[128,32,128]{2,1,0:T(8,128)(2,1)} %get-tuple-element.11), calls=%async_computation.1 | async-start | bytes 2097152 | tf_op jit(solution)/shard_map/all_to_all | solution.py:263
  174.4 78.4 %all-to-all-start.3 = ((bf16[128,3,32,128]{3,2,1,0:T(8,128)(2,1)}), bf16[128,3,32,128]{3,2,1,0:T(8,128)(2,1)}, u32[]{:S(2)}, u32[]{:S(2)}) async-start(bf16[128,3,32,128]{3,2,1,0:T(8,128)(2,1)} %cluster_backward.1), calls=%async_computation.3 | async-start | bytes 6291456 | tf_op jit(solution)/shard_map/all_to_all | solution.py:263
  195.4 2.4 collective-permute-start

commit v2 on v0

v2 whole, which is shorter than its diff:
```python
import jax
import jax.numpy as jnp
from jax import lax
from jax.experimental import pallas as pl
from jax.experimental.pallas import tpu as pltpu
from jax.sharding import PartitionSpec as P

CLUSTERS = 256
MOST = 2
DH = 128
SEQ = 128
HEADS = 8
TOK = 384
D = 2048
PER_HEAD = CLUSTERS * MOST
OWNERS = SEQ // HEADS
OWNED = CLUSTERS // OWNERS
ROWS = OWNED * MOST
SLOTS = SEQ * MOST
GROUP = 8
PAIR = 2
EMPTY = 64.0
NEGATIVE = -1e30
SCALE = DH ** -0.5
F32 = jnp.float32
BF16 = jnp.bfloat16

NT = ((1,), (1,))
NN = ((1,), (0,))
TN = ((0,), (0,))


def matmul(a, b, dims=NN):
    return lax.dot_general(a, b, (dims, ((), ())), preferred_element_type=F32)


def iota(shape, dim):
    return lax.broadcasted_iota(jnp.int32, shape, dim)


def dispatch_kernel(ids_ref, q_ref, k_ref, v_ref, og_ref, w_ref, out_ref):
    grad = matmul(og_ref[...], w_ref[...], NT).astype(BF16)
    before = jnp.where(iota((TOK, TOK), 0) < iota((TOK, TOK), 1), 1.0, 0.0).astype(BF16)
    for i in range(PAIR):
        lanes = slice(i * DH, (i + 1) * DH)
        owners = slice(i * OWNERS, (i + 1) * OWNERS)
        hit = jnp.where(iota((CLUSTERS, TOK), 0) == ids_ref[i], 1.0, 0.0)
        earlier = matmul(hit.astype(BF16), before)
        whole = jnp.concatenate([q_ref[:, lanes], k_ref[:, lanes], v_ref[:, lanes], grad[:, lanes]], axis=1)
        for m in range(MOST):
            mask = jnp.where(earlier == m, hit, 0.0)
            got = matmul(mask.astype(BF16), whole)
            used = jnp.sum(mask, axis=1, keepdims=True)
            rows = slice(m * OWNED, (m + 1) * OWNED)
            for j in range(4):
                part = got[:, j * DH : (j + 1) * DH]
                if j == 1:
                    part = part + EMPTY * (1.0 - used)
                out_ref[owners, j, rows, :] = part.astype(BF16).reshape(OWNERS, OWNED, DH)


def dispatch(ids, q, k, v, out_grad, weight):
    tokens = pl.BlockSpec((TOK, PAIR * DH), lambda h: (0, h))
    return pl.pallas_call(
        dispatch_kernel,
        grid=(HEADS // PAIR,),
        in_specs=[
            pl.BlockSpec((PAIR, 1, TOK), lambda h: (h, 0, 0)),
            tokens,
            tokens,
            tokens,
            pl.BlockSpec((TOK, D), lambda h: (0, 0)),
            pl.BlockSpec((PAIR * DH, D), lambda h: (h, 0)),
        ],
        out_specs=pl.BlockSpec((PAIR * OWNERS, 4, ROWS, DH), lambda h: (h, 0, 0, 0)),
        out_shape=jax.ShapeDtypeStruct((SEQ, 4, ROWS, DH), BF16),
        name="dispatch",
    )(ids, q, k, v, out_grad, weight)


def masks_kernel(idr_ref, idc_ref, out_ref):
    row, col = idr_ref[0], idc_ref[0]
    t, u = iota((TOK, TOK), 0), iota((TOK, TOK), 1)
    same = jnp.logical_and(col == row, u < t)
    earlier = jnp.max(jnp.where(same, 1, 0), axis=1, keepdims=True)
    slot = (col // OWNED) * ROWS + earlier * OWNED + col % OWNED
    out_ref[0] = jnp.where(iota((TOK, PER_HEAD), 1) == slot, 1.0, 0.0).astype(BF16)


def token_masks(idr, idc):
    return pl.pallas_call(
        masks_kernel,
        grid=(HEADS,),
        in_specs=[
            pl.BlockSpec((1, 1, TOK), lambda h: (h, 0, 0)),
            pl.BlockSpec((1, TOK, 1), lambda h: (h, 0, 0)),
        ],
        out_specs=pl.BlockSpec((1, TOK, PER_HEAD), lambda h: (h, 0, 0)),
        out_shape=jax.ShapeDtypeStruct((HEADS, TOK, PER_HEAD), BF16),
        name="token_masks",
    )(idr, idc)


PB = GROUP * ROWS
PER = GROUP * MOST


def regroup_matrix(inverse):
    a = iota((PB, PB), 1 if inverse else 0)
    b = iota((PB, PB), 0 if inverse else 1)
    want = ((a % PER) // MOST) * ROWS + (a % MOST) * OWNED + a // PER
    return jnp.where(b == want, 1.0, 0.0).astype(BF16)


def owner_kernel(in_ref, out_ref, q_ref, k_ref, v_ref, g_ref, o_ref, dq_ref, dk_ref, dv_ref):
    parts = (q_ref, k_ref, v_ref, g_ref)
    results = (o_ref, dq_ref, dk_ref, dv_ref)
    perm = regroup_matrix(False)
    for s in range(SEQ // GROUP):
        src = slice(s * GROUP, (s + 1) * GROUP)
        dst = slice(s * PER, (s + 1) * PER)
        whole = jnp.concatenate([in_ref[src, j].reshape(PB, DH) for j in range(4)], axis=1)
        got = matmul(perm, whole).astype(BF16)
        for j in range(4):
            parts[j][:, dst, :] = got[:, j * DH : (j + 1) * DH].reshape(OWNED, PER, DH)

    causal = iota((SLOTS, SLOTS), 0) <= iota((SLOTS, SLOTS), 1)

    def one(c):
        q, k, v, g = q_ref[c], k_ref[c], v_ref[c], g_ref[c]
        scores = matmul(k, q, NT) * SCALE
        allowed = jnp.logical_and(causal, k[:, 0:1].astype(F32) < 0.5 * EMPTY)
        scores = jnp.where(allowed, scores, NEGATIVE)
        weights = jnp.exp(scores - jnp.max(scores, axis=0, keepdims=True))
        probs = weights * (1.0 / jnp.sum(weights, axis=0, keepdims=True))
        half = probs.astype(BF16)
        dprob = matmul(v, g, NT)
        delta = jnp.sum(probs * dprob, axis=0, keepdims=True)
        ds = (probs * (dprob - delta)).astype(BF16)
        o_ref[c] = matmul(half, v, TN).astype(BF16)
        dv_ref[c] = matmul(half, g).astype(BF16)
        dk_ref[c] = (matmul(ds, q) * SCALE).astype(BF16)
        dq_ref[c] = (matmul(ds, k, TN) * SCALE).astype(BF16)

    def step(i, carry):
        one(2 * i)
        one(2 * i + 1)
        return carry

    lax.fori_loop(0, OWNED // 2, step, 0)
    back = regroup_matrix(True)
    for s in range(SEQ // GROUP):
        src = slice(s * GROUP, (s + 1) * GROUP)
        dst = slice(s * PER, (s + 1) * PER)
        whole = jnp.concatenate([r[:, dst, :].reshape(PB, DH) for r in results], axis=1)
        got = matmul(back, whole).astype(BF16)
        for j in range(4):
            out_ref[src, j] = got[:, j * DH : (j + 1) * DH].reshape(GROUP, ROWS, DH)


VM = pl.BlockSpec(memory_space=pltpu.VMEM)


def owner(received):
    return pl.pallas_call(
        owner_kernel,
        in_specs=[VM],
        out_specs=VM,
        out_shape=jax.ShapeDtypeStruct((SEQ, 4, ROWS, DH), BF16),
        scratch_shapes=[pltpu.VMEM((OWNED, SLOTS, DH), BF16)] * 8,
        name="owner",
    )(received)


def attn_kernel(core_ref, mask_ref, in_ref, w_ref, attn_ref, other_ref, acc_ref):
    h = pl.program_id(0)
    for i in range(PAIR):
        rows = in_ref[i * OWNERS : (i + 1) * OWNERS, 0].reshape(PER_HEAD, DH)
        attn_ref[:, i * DH : (i + 1) * DH] = matmul(mask_ref[i], rows).astype(BF16)
    part = matmul(attn_ref[...], w_ref[...])

    @pl.when(h == 0)
    def _():
        acc_ref[...] = part

    @pl.when(h > 0)
    def _():
        acc_ref[...] += part

    @pl.when(h == HEADS // PAIR - 1)
    def _():
        other_ref[...] = acc_ref[...].astype(BF16)


def attn_combine(core, masks, received, weight):
    return pl.pallas_call(
        attn_kernel,
        grid_spec=pltpu.PrefetchScalarGridSpec(
            num_scalar_prefetch=1,
            grid=(HEADS // PAIR,),
            in_specs=[
                pl.BlockSpec((PAIR, TOK, PER_HEAD), lambda h, core: (h, 0, 0)),
                pl.BlockSpec((PAIR * OWNERS, 1, ROWS, DH), lambda h, core: (h, 0, 0, 0)),
                pl.BlockSpec((PAIR * DH, D // 2), lambda h, core: (h, 1 - core[0])),
            ],
            out_specs=[
                pl.BlockSpec((TOK, PAIR * DH), lambda h, core: (0, h)),
                pl.BlockSpec((TOK, D // 2), lambda h, core: (0, 0)),
            ],
            scratch_shapes=[pltpu.VMEM((TOK, D // 2), F32)],
        ),
        out_shape=[
            jax.ShapeDtypeStruct((TOK, HEADS * DH), BF16),
            jax.ShapeDtypeStruct((TOK, D // 2), BF16),
        ],
        name="attn_combine",
    )(core, masks, received, weight)


def grads_kernel(mask_ref, in_ref, dq_ref, dk_ref, dv_ref):
    for i in range(PAIR):
        lanes = slice(i * DH, (i + 1) * DH)
        owners = slice(i * OWNERS, (i + 1) * OWNERS)
        whole = jnp.concatenate([in_ref[owners, j].reshape(PER_HEAD, DH) for j in (1, 2, 3)], axis=1)
        got = matmul(mask_ref[i], whole).astype(BF16)
        dq_ref[:, lanes] = got[:, :DH]
        dk_ref[:, lanes] = got[:, DH : 2 * DH]
        dv_ref[:, lanes] = got[:, 2 * DH :]


def grads_combine(masks, received):
    return pl.pallas_call(
        grads_kernel,
        grid=(HEADS // PAIR,),
        in_specs=[
            pl.BlockSpec((PAIR, TOK, PER_HEAD), lambda h: (h, 0, 0)),
            pl.BlockSpec((PAIR * OWNERS, 4, ROWS, DH), lambda h: (h, 0, 0, 0)),
        ],
        out_specs=[pl.BlockSpec((TOK, PAIR * DH), lambda h: (0, h))] * 3,
        out_shape=[jax.ShapeDtypeStruct((TOK, HEADS * DH), BF16)] * 3,
        name="grads_combine",
    )(masks, received)


def own_half_kernel(core_ref, attn_ref, w_ref, came_ref, out_ref):
    mine = matmul(attn_ref[...], w_ref[...])
    out_ref[...] = (mine + came_ref[...].astype(F32)).astype(BF16)


def own_half(core, attn, weight, came):
    width = 256
    steps = D // 2 // width
    return pl.pallas_call(
        own_half_kernel,
        grid_spec=pltpu.PrefetchScalarGridSpec(
            num_scalar_prefetch=1,
            grid=(steps,),
            in_specs=[
                pl.BlockSpec((TOK, HEADS * DH), lambda n, core: (0, 0)),
                pl.BlockSpec((HEADS * DH, width), lambda n, core: (0, core[0] * steps + n)),
                pl.BlockSpec((TOK, width), lambda n, core: (0, n)),
            ],
            out_specs=pl.BlockSpec((TOK, width), lambda n, core: (0, n)),
        ),
        out_shape=jax.ShapeDtypeStruct((TOK, D // 2), BF16),
        name="own_half",
    )(core, attn, weight, came)


def exchange(x):
    return lax.all_to_all(x, "seq", split_axis=0, concat_axis=0, tiled=True)


def body(query_rows, key_rows, value_rows, out_grad, cluster_ids, out_weight):
    idr = jnp.transpose(cluster_ids, (0, 2, 1))
    core = lax.axis_index("head").astype(jnp.int32).reshape(1)
    masks = token_masks(idr, cluster_ids)
    received = exchange(dispatch(idr, query_rows, key_rows, value_rows, out_grad, out_weight))
    back = exchange(owner(received))
    attn, other = attn_combine(core, masks, back, out_weight)
    came = lax.ppermute(other, "head", [(0, 1), (1, 0)])
    dq, dk, dv = grads_combine(masks, back)
    layer_out = own_half(core, attn, out_weight, came)
    return layer_out, dq, dk, dv


def solution(mesh):
    in_specs = (
        P("seq", "head"),
        P("seq", "head"),
        P("seq", "head"),
        P("seq", None),
        P("head", "seq", None),
        P("head", None),
    )
    out_specs = (P("seq", "head"), P("seq", "head"), P("seq", "head"), P("seq", "head"))
    return jax.shard_map(body, mesh=mesh, in_specs=in_specs, out_specs=out_specs, check_vma=False)
```

time: 406 us -> 266 us (0.66); the launches traced: 398 us -> 263 us
  local copies, waits for them, and re-layouts: 170 us -> 2.59 us
  blocking collectives: 0 us -> 114 us
  Pallas kernels: 0 us -> 50.9 us
  waiting for transfers between devices: 136 us -> 87 us
  starting transfers between devices: 45.9 us -> 7.91 us
  other arithmetic: 16.5 us -> 0 us
  matrix products: 15.6 us -> 0 us
  between operations: 14.6 us -> 0.66 us
    all_to_all x0 -> x1, blocking collectives: none -> 114 us  [exchange(): return lax.all_to_all(x, 'seq', split_axis=0, concat_axis=0, tiled=True)]
    gather x5 -> x0, local copies, waits for them, and re-layouts: 93.7 us -> none  [take_one(): return table[index_one]]
    pallas_call x0 -> x6, Pallas kernels: none -> 50.9 us  [the longest x1 14.8 us: owner(): pl.pallas_call(owner_kernel, in_specs=[VM], out_specs=VM, out_shape=jax.S...]
    all_to_all x4 -> x1, waiting for transfers between devices: 136 us -> 87 us  [exchange(): return lax.all_to_all(x, 'seq', split_axis=0, concat_axis=0, tiled=True)]
    unnamed x25 -> x5, local copies, waits for them, and re-layouts: 40.6 us -> 2.59 us
    all_to_all x4 -> x1, starting transfers between devices: 45.7 us -> 7.9 us  [exchange(): return lax.all_to_all(x, 'seq', split_axis=0, concat_axis=0, tiled=True)]
    dot_general x8 -> x0, matrix products: 15.6 us -> none  [the longest x1 5.16 us: body(): jnp.dot(attn_local, out_weight, preferred_element_type=jnp.float32)]
    all_to_all x7 -> x0, local copies, waits for them, and re-layouts: 12.2 us -> none  [the longest x2 3.79 us: body(): lax.all_to_all(forward_send, 'seq', split_axis=2, concat_axis=3, tiled=True)]
  transfers between devices with their start and end apart: 5 -> 2, of which waited for: 3 -> 1; matrix products, arithmetic and copies ran while one was open for 42% -> 1% of each run, Pallas kernels for 0% -> 5%
where the time goes in v2:
time: 266 us; the launch traced here: 263 us
  blocking collectives  114 us (43%)
  waiting for transfers between devices  87 us (33%)
  Pallas kernels  50.9 us (19%)
  starting transfers between devices  7.91 us (3%)
    all_to_all x1, blocking collectives, exchange(): return lax.all_to_all(x, 'seq', split_axis=0, concat_axis=0, tiled=True)  114 us
    all_to_all x1, waiting for transfers between devices, exchange(): return lax.all_to_all(x, 'seq', split_axis=0, concat_axis=0, tiled=True)  87 us
    pallas_call x1, Pallas kernels, owner(): pl.pallas_call(owner_kernel, in_specs=[VM], out_specs=VM, out_shape=jax.S...  14.8 us
    pallas_call x1, Pallas kernels, dispatch(): pl.pallas_call(dispatch_kernel, grid=(HEADS // PAIR,), in_specs=[pl.Block...  11.5 us
    all_to_all x1, starting transfers between devices, exchange(): return lax.all_to_all(x, 'seq', split_axis=0, concat_axis=0, tiled=True)  7.9 us
    pallas_call x1, Pallas kernels, token_masks(): pl.pallas_call(masks_kernel, grid=(HEADS,), in_specs=[pl.BlockSpec((1, 1,...  7.64 us
    pallas_call x1, Pallas kernels, attn_combine(): pl.pallas_call(attn_kernel, grid_spec=pltpu.PrefetchScalarGridSpec(num_sc...  6.26 us
    pallas_call x1, Pallas kernels, grads_combine(): pl.pallas_call(grads_kernel, grid=(HEADS // PAIR,), in_specs=[pl.BlockSpe...  5.98 us
  transfers between devices with their start and end apart: 2, of which 1 were waited for; matrix products, arithmetic and copies ran while one was open for 1% of the time, Pallas kernels for 5%

profile of v2, /device:TPU:32, one launch (start us, length us, event | category | flops | bytes accessed | tf_op | source)
XLA Modules:
  0.0 262.9 jit_solution(10933957403259492892)
XLA Ops:
  0.6 11.5 %dispatch.1 = bf16[128,4,32,128]{3,2,1,0:T(8,128)(2,1)} custom-call(s32[8,1,384]{2,1,0:T(1,128)} %bitcast.2, bf16[384,1024]{1,0:T(8,128)(2,1)} %q_ref.1, bf16[384,1024]{1,0:T(8,128)(2,1)} %k_ref.1, bf16[384,1024]{1,0:T(8,128)(2,1)} %v_ref.1, bf16[384,2048]{1,0:T(8,128)(2,1)} %og_ref.1, bf16[1024,2048]{1,0:T(8,128)(2,1)} %w_ref.5), custom_call_target="tpu_custom_call" | custom-call | tf_op jit(solution)/shard_map/dispatch/pallas_call | solution.py:64
  12.2 113.9 %all_to_all.10.in_ref = bf16[128,4,32,128]{3,2,1,0:T(8,128)(2,1)} all-to-all(bf16[128,4,32,128]{3,2,1,0:T(8,128)(2,1)} %dispatch.1), channel_id=1, replica_groups=mesh['seq'=128,'head'=2] {'seq'}, dimensions={0} | all-to-all | bytes 8388608 | tf_op jit(solution)/shard_map/all_to_all | solution.py:271
  126.0 14.8 %owner.1 = bf16[128,4,32,128]{3,2,1,0:T(8,128)(2,1)} custom-call(bf16[128,4,32,128]{3,2,1,0:T(8,128)(2,1)} %all_to_all.10.in_ref), custom_call_target="tpu_custom_call" | custom-call | tf_op jit(solution)/shard_map/owner/pallas_call | solution.py:165
  140.9 0.0 copy-start.1
  140.9 7.9 %all-to-all-start.1 = ((bf16[128,4,32,128]{3,2,1,0:T(8,128)(2,1)}), bf16[128,4,32,128]{3,2,1,0:T(8,128)(2,1)}, u32[]{:S(2)}, u32[]{:S(2)}) async-start(bf16[128,4,32,128]{3,2,1,0:T(8,128)(2,1)} %owner.1), calls=%async_computation.1 | async-start | bytes 8388608 | tf_op jit(solution)/shard_map/all_to_all | solution.py:271
  148.8 0.0 copy-done.1
  148.8 1.7 copy.10.idc_ref
  150.5 7.6 %token_masks.1.mask_ref = bf16[8,384,512]{2,1,0:T(8,128)(2,1)} custom-call(s32[8,1,384]{2,1,0:T(1,128)} %bitcast.3, s32[8,384,1]{2,1,0:T(8,128)} %copy.10.idc_ref), custom_call_target="tpu_custom_call" | custom-call | tf_op jit(solution)/shard_map/token_masks/pallas_call | solution.py:91
  158.1 87.0 %all-to-all-done.1.in_ref = bf16[128,4,32,128]{3,2,1,0:T(8,128)(2,1)} async-done(((bf16[128,4,32,128]{3,2,1,0:T(8,128)(2,1)}), bf16[128,4,32,128]{3,2,1,0:T(8,128)(2,1)}, u32[]{:S(2)}, u32[]{:S(2)}) %all-to-all-start.1) | async-done | bytes 4194336 | tf_op jit(solution)/shard_map/all_to_all | solution.py:271
  245.1 6.3 %attn_combine.1 = (bf16[384,1024]{1,0:T(8,128)(2,1)}, bf16[384,1024]{1,0:T(8,128)(2,1)}) custom-call(s32[1]{0:T(128)} %bitcast.core_ref, bf16[8,384,512]{2,1,0:T(8,128)(2,1)} %token_masks.1.mask_ref, bf16[128,4,32,128]{3,2,1,0:T(8,128)(2,1)} %all-to-all-done.1.in_ref, bf16[1024,2048]{1,0:T(8,128)(2,1)} %w_ref.5), custom_call_target="tpu_custom_call" | custom-call | tf_op jit(solution)/shard_map/attn_combine/pallas_call | solution.py:196
  251.4 0.0 collective-permute-start
  251.4 6.0 %grads_combine.1 = (bf16[384,1024]{1,0:T(8,128)(2,1)}, bf16[384,1024]{1,0:T(8,128)(2,1)}, bf16[384,1024]{1,0:T(8,128)(2,1)}) custom-call(bf16[8,384,512]{2,1,0:T(8,128)(2,1)} %token_masks.1.mask_ref, bf16[128,4,32,128]{3,2,1,0:T(8,128)(2,1)} %all-to-all-done.1.in_ref), custom_call_target="tpu_custom_call" | custom-call | tf_op jit(solution)/shard_map/grads_combine/pallas_call | solution.py:232
  257.3 0.0 collective-permute-done.came_ref
  257.3 0.0 copy-start
  257.3 0.9 copy-done
  258.2 4.6 %own_half.1 = bf16[384,1024]{1,0:T(8,128)(2,1)} custom-call(s32[1]{0:T(128)} %bitcast.core_ref, bf16[384,1024]{1,0:T(8,128)(2,1)} %get-tuple-element.9.attn_ref, bf16[1024,2048]{1,0:T(8,128)(2,1)} %w_ref.5, bf16[384,1024]{1,0:T(8,128)(2,1)} %copy-done), custom_call_target="tpu_custom_call" | custom-call | tf_op jit(solution)/shard_map/own_half/pallas_call | solution.py:253
Async XLA Ops:
  140.9 7.9 %copy-start.1 = (s32[8,384,1]{1,2,0:T(1,128)S(1)}, s32[8,384,1]{1,2,0:T(1,128)}, u32[]{:S(2)}) copy-start(s32[8,384,1]{1,2,0:T(1,128)} %param.10) | copy-start | bytes 36868
  140.9 104.2 %all-to-all-start.1 = ((bf16[128,4,32,128]{3,2,1,0:T(8,128)(2,1)}), bf16[128,4,32,128]{3,2,1,0:T(8,128)(2,1)}, u32[]{:S(2)}, u32[]{:S(2)}) async-start(bf16[128,4,32,128]{3,2,1,0:T(8,128)(2,1)} %owner.1), calls=%async_computation.1 | async-start | bytes 8388608 | tf_op jit(solution)/shard_map/all_to_all | solution.py:271
  251.4 6.0 %collective-permute-start = (bf16[384,1024]{1,0:T(8,128)(2,1)}, bf16[384,1024]{1,0:T(8,128)(2,1)S(1)}, u32[]{:S(2)}, u32[]{:S(2)}) collective-permute-start(bf16[384,1024]{1,0:T(8,128)(2,1)} %get-tuple-element.10), channel_id=1, source_target_pairs={{0,1},{1,0},{2,3},{3,2},{4,5},{5,4},{6,7},{7,6},{8,9},{9,8},{10,11... | collective-permute-start | bytes 2359304 | tf_op jit(solution)/shard_map/ppermute | solution.py:281
  257.3 0.9 copy-start

commit v3 on v2

--- a/solution.py
+++ b/solution.py
@@ -38,44 +38,64 @@
     return lax.broadcasted_iota(jnp.int32, shape, dim)
 
 
-def dispatch_kernel(ids_ref, q_ref, k_ref, v_ref, og_ref, w_ref, out_ref):
-    grad = matmul(og_ref[...], w_ref[...], NT).astype(BF16)
+def send_masks(ids):
     before = jnp.where(iota((TOK, TOK), 0) < iota((TOK, TOK), 1), 1.0, 0.0).astype(BF16)
+    hit = jnp.where(iota((CLUSTERS, TOK), 0) == ids, 1.0, 0.0)
+    earlier = matmul(hit.astype(BF16), before)
+    return [jnp.where(earlier == m, hit, 0.0) for m in range(MOST)]
+
+
+def dispatch_kernel(ids_ref, q_ref, k_ref, v_ref, out_ref):
     for i in range(PAIR):
         lanes = slice(i * DH, (i + 1) * DH)
         owners = slice(i * OWNERS, (i + 1) * OWNERS)
-        hit = jnp.where(iota((CLUSTERS, TOK), 0) == ids_ref[i], 1.0, 0.0)
-        earlier = matmul(hit.astype(BF16), before)
-        whole = jnp.concatenate([q_ref[:, lanes], k_ref[:, lanes], v_ref[:, lanes], grad[:, lanes]], axis=1)
-        for m in range(MOST):
-            mask = jnp.where(earlier == m, hit, 0.0)
+        whole = jnp.concatenate([q_ref[:, lanes], k_ref[:, lanes], v_ref[:, lanes]], axis=1)
+        for m, mask in enumerate(send_masks(ids_ref[i])):
             got = matmul(mask.astype(BF16), whole)
             used = jnp.sum(mask, axis=1, keepdims=True)
             rows = slice(m * OWNED, (m + 1) * OWNED)
-            for j in range(4):
+            for j in range(3):
                 part = got[:, j * DH : (j + 1) * DH]
                 if j == 1:
                     part = part + EMPTY * (1.0 - used)
                 out_ref[owners, j, rows, :] = part.astype(BF16).reshape(OWNERS, OWNED, DH)
 
 
-def dispatch(ids, q, k, v, out_grad, weight):
+def grad_dispatch_kernel(ids_ref, og_ref, w_ref, out_ref):
+    grad = matmul(og_ref[...], w_ref[...], NT).astype(BF16)
+    for i in range(PAIR):
+        owners = slice(i * OWNERS, (i + 1) * OWNERS)
+        for m, mask in enumerate(send_masks(ids_ref[i])):
+            got = matmul(mask.astype(BF16), grad[:, i * DH : (i + 1) * DH])
+            rows = slice(m * OWNED, (m + 1) * OWNED)
+            out_ref[owners, 0, rows, :] = got.astype(BF16).reshape(OWNERS, OWNED, DH)
+
+
+def dispatch(ids, q, k, v):
     tokens = pl.BlockSpec((TOK, PAIR * DH), lambda h: (0, h))
     return pl.pallas_call(
         dispatch_kernel,
+        grid=(HEADS // PAIR,),
+        in_specs=[pl.BlockSpec((PAIR, 1, TOK), lambda h: (h, 0, 0)), tokens, tokens, tokens],
+        out_specs=pl.BlockSpec((PAIR * OWNERS, 3, ROWS, DH), lambda h: (h, 0, 0, 0)),
+        out_shape=jax.ShapeDtypeStruct((SEQ, 3, ROWS, DH), BF16),
+        name="dispatch",
+    )(ids, q, k, v)
+
+
+def grad_dispatch(ids, out_grad, weight):
+    return pl.pallas_call(
+        grad_dispatch_kernel,
         grid=(HEADS // PAIR,),
         in_specs=[
             pl.BlockSpec((PAIR, 1, TOK), lambda h: (h, 0, 0)),
-            tokens,
-            tokens,
-            tokens,
             pl.BlockSpec((TOK, D), lambda h: (0, 0)),
             pl.BlockSpec((PAIR * DH, D), lambda h: (h, 0)),
         ],
-        out_specs=pl.BlockSpec((PAIR * OWNERS, 4, ROWS, DH), lambda h: (h, 0, 0, 0)),
-        out_shape=jax.ShapeDtypeStruct((SEQ, 4, ROWS, DH), BF16),
-        name="dispatch",
-    )(ids, q, k, v, out_grad, weight)
+        out_specs=pl.BlockSpec((PAIR * OWNERS, 1, ROWS, DH), lambda h: (h, 0, 0, 0)),
+        out_shape=jax.ShapeDtypeStruct((SEQ, 1, ROWS, DH), BF16),
+        name="grad_dispatch",
+    )(ids, out_grad, weight)
 
 
 def masks_kernel(idr_ref, idc_ref, out_ref):
@@ -112,70 +132,106 @@
     return jnp.where(b == want, 1.0, 0.0).astype(BF16)
 
 
-def owner_kernel(in_ref, out_ref, q_ref, k_ref, v_ref, g_ref, o_ref, dq_ref, dk_ref, dv_ref):
-    parts = (q_ref, k_ref, v_ref, g_ref)
-    results = (o_ref, dq_ref, dk_ref, dv_ref)
+def each(count, unroll, fn):
+    def step(i, carry):
+        for n in range(unroll):
+            fn(i * unroll + n)
+        return carry
+
+    lax.fori_loop(0, count // unroll, step, 0)
+
+
+def regroup_in(in_ref, targets):
     perm = regroup_matrix(False)
+    width = len(targets)
     for s in range(SEQ // GROUP):
         src = slice(s * GROUP, (s + 1) * GROUP)
         dst = slice(s * PER, (s + 1) * PER)
-        whole = jnp.concatenate([in_ref[src, j].reshape(PB, DH) for j in range(4)], axis=1)
+        whole = jnp.concatenate([in_ref[src, j].reshape(PB, DH) for j in range(width)], axis=1)
         got = matmul(perm, whole).astype(BF16)
-        for j in range(4):
-            parts[j][:, dst, :] = got[:, j * DH : (j + 1) * DH].reshape(OWNED, PER, DH)
-
-    causal = iota((SLOTS, SLOTS), 0) <= iota((SLOTS, SLOTS), 1)
-
-    def one(c):
-        q, k, v, g = q_ref[c], k_ref[c], v_ref[c], g_ref[c]
-        scores = matmul(k, q, NT) * SCALE
-        allowed = jnp.logical_and(causal, k[:, 0:1].astype(F32) < 0.5 * EMPTY)
-        scores = jnp.where(allowed, scores, NEGATIVE)
-        weights = jnp.exp(scores - jnp.max(scores, axis=0, keepdims=True))
-        probs = weights * (1.0 / jnp.sum(weights, axis=0, keepdims=True))
-        half = probs.astype(BF16)
-        dprob = matmul(v, g, NT)
-        delta = jnp.sum(probs * dprob, axis=0, keepdims=True)
-        ds = (probs * (dprob - delta)).astype(BF16)
-        o_ref[c] = matmul(half, v, TN).astype(BF16)
-        dv_ref[c] = matmul(half, g).astype(BF16)
-        dk_ref[c] = (matmul(ds, q) * SCALE).astype(BF16)
-        dq_ref[c] = (matmul(ds, k, TN) * SCALE).astype(BF16)
-
-    def step(i, carry):
-        one(2 * i)
-        one(2 * i + 1)
-        return carry
-
-    lax.fori_loop(0, OWNED // 2, step, 0)
+        for j in range(width):
+            targets[j][:, dst, :] = got[:, j * DH : (j + 1) * DH].reshape(OWNED, PER, DH)
+
+
+def regroup_out(results, out_ref):
     back = regroup_matrix(True)
     for s in range(SEQ // GROUP):
         src = slice(s * GROUP, (s + 1) * GROUP)
         dst = slice(s * PER, (s + 1) * PER)
         whole = jnp.concatenate([r[:, dst, :].reshape(PB, DH) for r in results], axis=1)
         got = matmul(back, whole).astype(BF16)
-        for j in range(4):
+        for j in range(len(results)):
             out_ref[src, j] = got[:, j * DH : (j + 1) * DH].reshape(GROUP, ROWS, DH)
 
 
+def probabilities(q, k):
+    causal = iota((SLOTS, SLOTS), 0) <= iota((SLOTS, SLOTS), 1)
+    scores = matmul(k, q, NT) * SCALE
+    allowed = jnp.logical_and(causal, k[:, 0:1].astype(F32) < 0.5 * EMPTY)
+    scores = jnp.where(allowed, scores, NEGATIVE)
+    weights = jnp.exp(scores - jnp.max(scores, axis=0, keepdims=True))
+    return weights * (1.0 / jnp.sum(weights, axis=0, keepdims=True))
+
+
+def forward_kernel(in_ref, q_ref, k_ref, v_ref, out_ref, o_ref):
+    regroup_in(in_ref, (q_ref, k_ref, v_ref))
+
+    def one(c):
+        half = probabilities(q_ref[c], k_ref[c]).astype(BF16)
+        o_ref[c] = matmul(half, v_ref[c], TN).astype(BF16)
+
+    each(OWNED, 2, one)
+    regroup_out((o_ref,), out_ref)
+
+
+def backward_kernel(in_ref, q_ref, k_ref, v_ref, out_ref, g_ref, dq_ref, dk_ref, dv_ref):
+    regroup_in(in_ref, (g_ref,))
+
+    def one(c):
+        q, k, v, g = q_ref[c], k_ref[c], v_ref[c], g_ref[c]
+        probs = probabilities(q, k)
+        dprob = matmul(v, g, NT)
+        delta = jnp.sum(probs * dprob, axis=0, keepdims=True)
+        ds = (probs * (dprob - delta)).astype(BF16)
+        dv_ref[c] = matmul(probs.astype(BF16), g).astype(BF16)
+        dk_ref[c] = (matmul(ds, q) * SCALE).astype(BF16)
+        dq_ref[c] = (matmul(ds, k, TN) * SCALE).astype(BF16)
+
+    each(OWNED, 2, one)
+    regroup_out((dq_ref, dk_ref, dv_ref), out_ref)
+
+
 VM = pl.BlockSpec(memory_space=pltpu.VMEM)
-
-
-def owner(received):
-    return pl.pallas_call(
-        owner_kernel,
+GROUPED = (OWNED, SLOTS, DH)
+
+
+def forward(received):
+    return pl.pallas_call(
+        forward_kernel,
         in_specs=[VM],
+        out_specs=[VM] * 4,
+        out_shape=[jax.ShapeDtypeStruct(GROUPED, BF16)] * 3 + [jax.ShapeDtypeStruct((SEQ, 1, ROWS, DH), BF16)],
+        scratch_shapes=[pltpu.VMEM(GROUPED, BF16)],
+        name="cluster_forward",
+    )(received)
+
+
+def backward(received, q, k, v):
+    return pl.pallas_call(
+        backward_kernel,
+        in_specs=[VM] * 4,
         out_specs=VM,
-        out_shape=jax.ShapeDtypeStruct((SEQ, 4, ROWS, DH), BF16),
-        scratch_shapes=[pltpu.VMEM((OWNED, SLOTS, DH), BF16)] * 8,
-        name="owner",
-    )(received)
+        out_shape=jax.ShapeDtypeStruct((SEQ, 3, ROWS, DH), BF16),
+        scratch_shapes=[pltpu.VMEM(GROUPED, BF16)] * 4,
+        name="cluster_backward",
+    )(received, q, k, v)
 
 
 def attn_kernel(core_ref, mask_ref, in_ref, w_ref, attn_ref, other_ref, acc_ref):
     h = pl.program_id(0)
     for i in range(PAIR):
-        rows = in_ref[i * OWNERS : (i + 1) * OWNERS, 0].reshape(PER_HEAD, DH)
+        owners = pl.ds((h * PAIR + i) * OWNERS, OWNERS)
+        rows = in_ref[owners, 0].reshape(PER_HEAD, DH)
         attn_ref[:, i * DH : (i + 1) * DH] = matmul(mask_ref[i], rows).astype(BF16)
     part = matmul(attn_ref[...], w_ref[...])
 
@@ -200,7 +256,7 @@
             grid=(HEADS // PAIR,),
             in_specs=[
                 pl.BlockSpec((PAIR, TOK, PER_HEAD), lambda h, core: (h, 0, 0)),
-                pl.BlockSpec((PAIR * OWNERS, 1, ROWS, DH), lambda h, core: (h, 0, 0, 0)),
+                VM,
                 pl.BlockSpec((PAIR * DH, D // 2), lambda h, core: (h, 1 - core[0])),
             ],
             out_specs=[
@@ -220,8 +276,8 @@
 def grads_kernel(mask_ref, in_ref, dq_ref, dk_ref, dv_ref):
     for i in range(PAIR):
         lanes = slice(i * DH, (i + 1) * DH)
-        owners = slice(i * OWNERS, (i + 1) * OWNERS)
-        whole = jnp.concatenate([in_ref[owners, j].reshape(PER_HEAD, DH) for j in (1, 2, 3)], axis=1)
+        owners = pl.ds((pl.program_id(0) * PAIR + i) * OWNERS, OWNERS)
+        whole = jnp.concatenate([in_ref[owners, j].reshape(PER_HEAD, DH) for j in range(3)], axis=1)
         got = matmul(mask_ref[i], whole).astype(BF16)
         dq_ref[:, lanes] = got[:, :DH]
         dk_ref[:, lanes] = got[:, DH : 2 * DH]
@@ -234,7 +290,7 @@
         grid=(HEADS // PAIR,),
         in_specs=[
             pl.BlockSpec((PAIR, TOK, PER_HEAD), lambda h: (h, 0, 0)),
-            pl.BlockSpec((PAIR * OWNERS, 4, ROWS, DH), lambda h: (h, 0, 0, 0)),
+            VM,
         ],
         out_specs=[pl.BlockSpec((TOK, PAIR * DH), lambda h: (0, h))] * 3,
         out_shape=[jax.ShapeDtypeStruct((TOK, HEADS * DH), BF16)] * 3,
@@ -268,19 +324,23 @@
 
 
 def exchange(x):
-    return lax.all_to_all(x, "seq", split_axis=0, concat_axis=0, tiled=True)
+    got = lax.all_to_all(x, "seq", split_axis=0, concat_axis=0, tiled=True)
+    return pltpu.with_memory_space_constraint(got, pltpu.MemorySpace.VMEM)
 
 
 def body(query_rows, key_rows, value_rows, out_grad, cluster_ids, out_weight):
     idr = jnp.transpose(cluster_ids, (0, 2, 1))
     core = lax.axis_index("head").astype(jnp.int32).reshape(1)
     masks = token_masks(idr, cluster_ids)
-    received = exchange(dispatch(idr, query_rows, key_rows, value_rows, out_grad, out_weight))
-    back = exchange(owner(received))
-    attn, other = attn_combine(core, masks, back, out_weight)
+    received = exchange(dispatch(idr, query_rows, key_rows, value_rows))
+    grads_in = exchange(grad_dispatch(idr, out_grad, out_weight))
+    q, k, v, attn_out = forward(received)
+    attn_back = exchange(attn_out)
+    back = exchange(backward(grads_in, q, k, v))
+    attn, other = attn_combine(core, masks, attn_back, out_weight)
     came = lax.ppermute(other, "head", [(0, 1), (1, 0)])
+    layer_out = own_half(core, attn, out_weight, came)
     dq, dk, dv = grads_combine(masks, back)
-    layer_out = own_half(core, attn, out_weight, came)
     return layer_out, dq, dk, dv
 
 

time: 266 us -> 255 us (0.959)
  blocking collectives: 114 us -> 0 us
  waiting for transfers between devices: 87 us -> 151 us
  starting transfers between devices: 7.91 us -> 37 us
  Pallas kernels: 50.9 us -> 63.3 us
    all_to_all x1 -> x0, blocking collectives: 114 us -> none  [exchange(): return lax.all_to_all(x, 'seq', split_axis=0, concat_axis=0, tiled=True)]
    all_to_all x1 -> x4, waiting for transfers between devices: 87 us -> 148 us  [exchange(): got = lax.all_to_all(x, 'seq', split_axis=0, concat_axis=0, tiled=True)]
    all_to_all x1 -> x4, starting transfers between devices: 7.9 us -> 37 us  [exchange(): got = lax.all_to_all(x, 'seq', split_axis=0, concat_axis=0, tiled=True)]
    pallas_call x1 -> x3, Pallas kernels: 14.8 us -> 32.4 us  [the longest x1 13.4 us: backward(): pl.pallas_call(backward_kernel, in_specs=[VM] * 4, out_specs=VM, out_shap...]
    pallas_call x1, Pallas kernels: 11.5 us -> 6.49 us  [dispatch(): pl.pallas_call(dispatch_kernel, grid=(HEADS // PAIR,), in_specs=[pl.Block...]
  transfers between devices with their start and end apart: 2 -> 5, of which waited for: 1 -> 5; matrix products, arithmetic and copies ran while one was open for 1% -> 1% of each run, Pallas kernels for 5% -> 20%
where the time goes in v3:
time: 255 us; the launch traced here: 254 us
  waiting for transfers between devices  151 us (59%)
  Pallas kernels  63.3 us (25%)
  starting transfers between devices  37 us (15%)
    all_to_all x4, waiting for transfers between devices, exchange(): got = lax.all_to_all(x, 'seq', split_axis=0, concat_axis=0, tiled=True)  148 us
    all_to_all x4, starting transfers between devices, exchange(): got = lax.all_to_all(x, 'seq', split_axis=0, concat_axis=0, tiled=True)  37 us
    pallas_call x1, Pallas kernels, backward(): pl.pallas_call(backward_kernel, in_specs=[VM] * 4, out_specs=VM, out_shap...  13.4 us
    pallas_call x1, Pallas kernels, forward(): pl.pallas_call(forward_kernel, in_specs=[VM], out_specs=[VM] * 4, out_sha...  9.56 us
    pallas_call x1, Pallas kernels, grad_dispatch(): pl.pallas_call(grad_dispatch_kernel, grid=(HEADS // PAIR,), in_specs=[pl....  9.44 us
    pallas_call x1, Pallas kernels, token_masks(): pl.pallas_call(masks_kernel, grid=(HEADS,), in_specs=[pl.BlockSpec((1, 1,...  7.64 us
    pallas_call x1, Pallas kernels, dispatch(): pl.pallas_call(dispatch_kernel, grid=(HEADS // PAIR,), in_specs=[pl.Block...  6.49 us
    pallas_call x1, Pallas kernels, grads_combine(): pl.pallas_call(grads_kernel, grid=(HEADS // PAIR,), in_specs=[pl.BlockSpe...  6.11 us
  transfers between devices with their start and end apart: 5, of which 5 were waited for; matrix products, arithmetic and copies ran while one was open for 1% of the time, Pallas kernels for 20%

profile of v3, /device:TPU:32, one launch (start us, length us, event | category | flops | bytes accessed | tf_op | source)
XLA Modules:
  0.0 254.4 jit_solution(6869026650584287193)
XLA Ops:
  0.6 6.5 %dispatch.1 = bf16[128,3,32,128]{3,2,1,0:T(8,128)(2,1)} custom-call(s32[8,1,384]{2,1,0:T(1,128)} %bitcast.2, bf16[384,1024]{1,0:T(8,128)(2,1)} %q_ref.1, bf16[384,1024]{1,0:T(8,128)(2,1)} %k_ref.1, bf16[384,1024]{1,0:T(8,128)(2,1)} %v_ref.1), custom_call_target="tpu_custom_call" | custom-call | tf_op jit(solution)/shard_map/dispatch/pallas_call | solution.py:76
  7.1 15.0 %all-to-all-start = ((bf16[128,3,32,128]{3,2,1,0:T(8,128)(2,1)}), bf16[128,3,32,128]{3,2,1,0:T(8,128)(2,1)S(1)}, u32[]{:S(2)}, u32[]{:S(2)}) async-start(bf16[128,3,32,128]{3,2,1,0:T(8,128)(2,1)} %dispatch.1), calls=%async_computation | async-start | bytes 6291456 | tf_op jit(solution)/shard_map/all_to_all | solution.py:327
  22.1 9.4 %grad_dispatch.1 = bf16[128,1,32,128]{3,2,1,0:T(8,128)(2,1)} custom-call(s32[8,1,384]{2,1,0:T(1,128)} %bitcast.3, bf16[384,2048]{1,0:T(8,128)(2,1)} %og_ref.1, bf16[1024,2048]{1,0:T(8,128)(2,1)} %w_ref.5), custom_call_target="tpu_custom_call" | custom-call | tf_op jit(solution)/shard_map/grad_dispatch/pallas_call | solution.py:87
  31.6 66.9 %all-to-all-done.in_ref = bf16[128,3,32,128]{3,2,1,0:T(8,128)(2,1)S(1)} async-done(((bf16[128,3,32,128]{3,2,1,0:T(8,128)(2,1)}), bf16[128,3,32,128]{3,2,1,0:T(8,128)(2,1)S(1)}, u32[]{:S(2)}, u32[]{:S(2)}) %all-to-all-start) | async-done | bytes 3145760 | tf_op jit(solution)/shard_map/all_to_all | solution.py:327
  98.4 7.7 %all-to-all-start.2 = ((bf16[128,1,32,128]{3,2,1,0:T(8,128)(2,1)}), bf16[128,1,32,128]{3,2,1,0:T(8,128)(2,1)}, u32[]{:S(2)}, u32[]{:S(2)}) async-start(bf16[128,1,32,128]{3,2,1,0:T(8,128)(2,1)} %grad_dispatch.1), calls=%async_computation.2 | async-start | bytes 2097152 | tf_op jit(solution)/shard_map/all_to_all | solution.py:327
  106.1 9.6 %cluster_forward.1 = (bf16[16,256,128]{2,1,0:T(8,128)(2,1)}, bf16[16,256,128]{2,1,0:T(8,128)(2,1)}, bf16[16,256,128]{2,1,0:T(8,128)(2,1)}, bf16[128,1,32,128]{3,2,1,0:T(8,128)(2,1)}) custom-call(bf16[128,3,32,128]{3,2,1,0:T(8,128)(2,1)S(1)} %all-to-all-done.in_ref), custom_call_target="tpu_custom_call" | custom-call | tf_op jit(solution)/shard_map/cluster_forward/pallas_call | solution.py:209
  115.7 19.7 %all-to-all-done.2.in_ref = bf16[128,1,32,128]{3,2,1,0:T(8,128)(2,1)} async-done(((bf16[128,1,32,128]{3,2,1,0:T(8,128)(2,1)}), bf16[128,1,32,128]{3,2,1,0:T(8,128)(2,1)}, u32[]{:S(2)}, u32[]{:S(2)}) %all-to-all-start.2) | async-done | bytes 1048608 | tf_op jit(solution)/shard_map/all_to_all | solution.py:327
  135.4 6.6 %all-to-all-start.1 = ((bf16[128,1,32,128]{3,2,1,0:T(8,128)(2,1)}), bf16[128,1,32,128]{3,2,1,0:T(8,128)(2,1)S(1)}, u32[]{:S(2)}, u32[]{:S(2)}) async-start(bf16[128,1,32,128]{3,2,1,0:T(8,128)(2,1)} %get-tuple-element.13), calls=%async_computation.1 | async-start | bytes 2097152 | tf_op jit(solution)/shard_map/all_to_all | solution.py:327
  142.0 13.4 %cluster_backward.1 = bf16[128,3,32,128]{3,2,1,0:T(8,128)(2,1)} custom-call(bf16[128,1,32,128]{3,2,1,0:T(8,128)(2,1)} %all-to-all-done.2.in_ref, bf16[16,256,128]{2,1,0:T(8,128)(2,1)} %get-tuple-element.16.q_ref, bf16[16,256,128]{2,1,0:T(8,128)(2,1)} %get-tuple-element.17.k_ref, bf16[16,256,128]{2,1,0:T(8,128)(2,1)} %get-tuple-element.18.v_ref), custom_call_target="tpu_custom_call" | custom-call | tf_op jit(solution)/shard_map/cluster_backward/pallas_call | solution.py:220
  155.4 0.0 copy-start.1
  155.4 14.4 %all-to-all-done.1.in_ref = bf16[128,1,32,128]{3,2,1,0:T(8,128)(2,1)S(1)} async-done(((bf16[128,1,32,128]{3,2,1,0:T(8,128)(2,1)}), bf16[128,1,32,128]{3,2,1,0:T(8,128)(2,1)S(1)}, u32[]{:S(2)}, u32[]{:S(2)}) %all-to-all-start.1) | async-done | bytes 1048608 | tf_op jit(solution)/shard_map/all_to_all | solution.py:327
  169.9 7.7 %all-to-all-start.3 = ((bf16[128,3,32,128]{3,2,1,0:T(8,128)(2,1)}), bf16[128,3,32,128]{3,2,1,0:T(8,128)(2,1)}, u32[]{:S(2)}, u32[]{:S(2)}) async-start(bf16[128,3,32,128]{3,2,1,0:T(8,128)(2,1)} %cluster_backward.1), calls=%async_computation.3 | async-start | bytes 6291456 | tf_op jit(solution)/shard_map/all_to_all | solution.py:327
  177.5 0.0 copy-done.1
  177.6 1.7 copy.10.idc_ref
  179.2 7.6 %token_masks.1.mask_ref = bf16[8,384,512]{2,1,0:T(8,128)(2,1)} custom-call(s32[8,1,384]{2,1,0:T(1,128)} %bitcast.4, s32[8,384,1]{2,1,0:T(8,128)} %copy.10.idc_ref), custom_call_target="tpu_custom_call" | custom-call | tf_op jit(solution)/shard_map/token_masks/pallas_call | solution.py:111
  186.9 6.1 %attn_combine.1 = (bf16[384,1024]{1,0:T(8,128)(2,1)}, bf16[384,1024]{1,0:T(8,128)(2,1)}) custom-call(s32[1]{0:T(128)} %bitcast.core_ref, bf16[8,384,512]{2,1,0:T(8,128)(2,1)} %token_masks.1.mask_ref, bf16[128,1,32,128]{3,2,1,0:T(8,128)(2,1)S(1)} %all-to-all-done.1.in_ref, bf16[1024,2048]{1,0:T(8,128)(2,1)} %w_ref.5), custom_call_target="tpu_custom_call" | custom-call | tf_op jit(solution)/shard_map/attn_combine/pallas_call | solution.py:252
  192.9 0.0 collective-permute-start
  192.9 2.5 collective-permute-done.came_ref
  195.4 0.0 copy-start
  195.4 0.9 copy-done
  196.3 4.6 %own_half.1 = bf16[384,1024]{1,0:T(8,128)(2,1)} custom-call(s32[1]{0:T(128)} %bitcast.core_ref, bf16[384,1024]{1,0:T(8,128)(2,1)} %get-tuple-element.14.attn_ref, bf16[1024,2048]{1,0:T(8,128)(2,1)} %w_ref.5, bf16[384,1024]{1,0:T(8,128)(2,1)} %copy-done), custom_call_target="tpu_custom_call" | custom-call | tf_op jit(solution)/shard_map/own_half/pallas_call | solution.py:309
  200.9 47.4 %all-to-all-done.3.in_ref = bf16[128,3,32,128]{3,2,1,0:T(8,128)(2,1)} async-done(((bf16[128,3,32,128]{3,2,1,0:T(8,128)(2,1)}), bf16[128,3,32,128]{3,2,1,0:T(8,128)(2,1)}, u32[]{:S(2)}, u32[]{:S(2)}) %all-to-all-start.3) | async-done | bytes 3145760 | tf_op jit(solution)/shard_map/all_to_all | solution.py:327
  248.3 6.1 %grads_combine.1 = (bf16[384,1024]{1,0:T(8,128)(2,1)}, bf16[384,1024]{1,0:T(8,128)(2,1)}, bf16[384,1024]{1,0:T(8,128)(2,1)}) custom-call(bf16[8,384,512]{2,1,0:T(8,128)(2,1)} %token_masks.1.mask_ref, bf16[128,3,32,128]{3,2,1,0:T(8,128)(2,1)} %all-to-all-done.3.in_ref), custom_call_target="tpu_custom_call" | custom-call | tf_op jit(solution)/shard_map/grads_combine/pallas_call | solution.py:288
Async XLA Ops:
  7.1 91.3 %all-to-all-start = ((bf16[128,3,32,128]{3,2,1,0:T(8,128)(2,1)}), bf16[128,3,32,128]{3,2,1,0:T(8,128)(2,1)S(1)}, u32[]{:S(2)}, u32[]{:S(2)}) async-start(bf16[128,3,32,128]{3,2,1,0:T(8,128)(2,1)} %dispatch.1), calls=%async_computation | async-start | bytes 6291456 | tf_op jit(solution)/shard_map/all_to_all | solution.py:327
  98.4 36.9 %all-to-all-start.2 = ((bf16[128,1,32,128]{3,2,1,0:T(8,128)(2,1)}), bf16[128,1,32,128]{3,2,1,0:T(8,128)(2,1)}, u32[]{:S(2)}, u32[]{:S(2)}) async-start(bf16[128,1,32,128]{3,2,1,0:T(8,128)(2,1)} %grad_dispatch.1), calls=%async_computation.2 | async-start | bytes 2097152 | tf_op jit(solution)/shard_map/all_to_all | solution.py:327
  135.4 34.5 %all-to-all-start.1 = ((bf16[128,1,32,128]{3,2,1,0:T(8,128)(2,1)}), bf16[128,1,32,128]{3,2,1,0:T(8,128)(2,1)S(1)}, u32[]{:S(2)}, u32[]{:S(2)}) async-start(bf16[128,1,32,128]{3,2,1,0:T(8,128)(2,1)} %get-tuple-element.13), calls=%async_computation.1 | async-start | bytes 2097152 | tf_op jit(solution)/shard_map/all_to_all | solution.py:327
  155.4 22.1 %copy-start.1 = (s32[8,384,1]{1,2,0:T(1,128)S(1)}, s32[8,384,1]{1,2,0:T(1,128)}, u32[]{:S(2)}) copy-start(s32[8,384,1]{1,2,0:T(1,128)} %param.10) | copy-start | bytes 36868
  169.9 78.4 %all-to-all-start.3 = ((bf16[128,3,32,128]{3,2,1,0:T(8,128)(2,1)}), bf16[128,3,32,128]{3,2,1,0:T(8,128)(2,1)}, u32[]{:S(2)}, u32[]{:S(2)}) async-start(bf16[128,3,32,128]{3,2,1,0:T(8,128)(2,1)} %cluster_backward.1), calls=%async_computation.3 | async-start | bytes 6291456 | tf_op jit(solution)/shard_map/all_to_all | solution.py:327
  192.9 2.5 collective-permute-start
  195.4 0.9 copy-start

commit v4 on v3

--- a/solution.py
+++ b/solution.py
@@ -19,12 +19,17 @@
 SLOTS = SEQ * MOST
 GROUP = 8
 PAIR = 2
+STEP = 4
+PARTS = 4
 EMPTY = 64.0
 NEGATIVE = -1e30
 SCALE = DH ** -0.5
 F32 = jnp.float32
 BF16 = jnp.bfloat16
 
+VM = pl.BlockSpec(memory_space=pltpu.VMEM)
+ANY = pl.BlockSpec(memory_space=pl.ANY)
+
 NT = ((1,), (1,))
 NN = ((1,), (0,))
 TN = ((0,), (0,))
@@ -45,57 +50,60 @@
     return [jnp.where(earlier == m, hit, 0.0) for m in range(MOST)]
 
 
-def dispatch_kernel(ids_ref, q_ref, k_ref, v_ref, out_ref):
-    for i in range(PAIR):
-        lanes = slice(i * DH, (i + 1) * DH)
-        owners = slice(i * OWNERS, (i + 1) * OWNERS)
-        whole = jnp.concatenate([q_ref[:, lanes], k_ref[:, lanes], v_ref[:, lanes]], axis=1)
-        for m, mask in enumerate(send_masks(ids_ref[i])):
-            got = matmul(mask.astype(BF16), whole)
-            used = jnp.sum(mask, axis=1, keepdims=True)
-            rows = slice(m * OWNED, (m + 1) * OWNED)
-            for j in range(3):
-                part = got[:, j * DH : (j + 1) * DH]
-                if j == 1:
-                    part = part + EMPTY * (1.0 - used)
-                out_ref[owners, j, rows, :] = part.astype(BF16).reshape(OWNERS, OWNED, DH)
-
-
-def grad_dispatch_kernel(ids_ref, og_ref, w_ref, out_ref):
-    grad = matmul(og_ref[...], w_ref[...], NT).astype(BF16)
-    for i in range(PAIR):
-        owners = slice(i * OWNERS, (i + 1) * OWNERS)
-        for m, mask in enumerate(send_masks(ids_ref[i])):
-            got = matmul(mask.astype(BF16), grad[:, i * DH : (i + 1) * DH])
-            rows = slice(m * OWNED, (m + 1) * OWNED)
-            out_ref[owners, 0, rows, :] = got.astype(BF16).reshape(OWNERS, OWNED, DH)
-
-
-def dispatch(ids, q, k, v):
-    tokens = pl.BlockSpec((TOK, PAIR * DH), lambda h: (0, h))
+def dispatch_kernel(ids_ref, q_hbm, k_hbm, v_hbm, og_hbm, w_hbm, out_hbm, q_ref, k_ref, v_ref, og_ref, w_ref, buf_ref, mask_ref, in_sem, w_sem, out_sem):
+    half = STEP * DH
+    ins = [pltpu.make_async_copy(a, b, in_sem.at[i]) for i, (a, b) in enumerate(((og_hbm, og_ref), (q_hbm, q_ref), (k_hbm, k_ref), (v_hbm, v_ref)))]
+    ws = [pltpu.make_async_copy(w_hbm.at[pl.ds(n * half, half)], w_ref.at[pl.ds(n * half, half)], w_sem.at[n]) for n in range(HEADS // STEP)]
+    ins[0].start()
+    ws[0].start()
+    for c in ins[1:]:
+        c.start()
+    for c in ws[1:]:
+        c.start()
+    for h in range(HEADS):
+        for m, mask in enumerate(send_masks(ids_ref[h])):
+            mask_ref[h, m] = mask.astype(BF16)
+    ins[0].wait()
+    outs = []
+    for n in range(HEADS // STEP):
+        ws[n].wait()
+        grad = matmul(og_ref[...], w_ref[n * half : (n + 1) * half], NT).astype(BF16)
+        if n == 0:
+            for c in ins[1:]:
+                c.wait()
+        for i in range(STEP):
+            h = n * STEP + i
+            lanes = slice(h * DH, (h + 1) * DH)
+            owners = slice(h * OWNERS, (h + 1) * OWNERS)
+            whole = jnp.concatenate([q_ref[:, lanes], k_ref[:, lanes], v_ref[:, lanes], grad[:, i * DH : (i + 1) * DH]], axis=1)
+            for m in range(MOST):
+                mask = mask_ref[h, m]
+                got = matmul(mask, whole)
+                used = jnp.sum(mask.astype(F32), axis=1, keepdims=True)
+                rows = slice(m * OWNED, (m + 1) * OWNED)
+                for j in range(4):
+                    part = got[:, j * DH : (j + 1) * DH]
+                    if j == 1:
+                        part = part + EMPTY * (1.0 - used)
+                    buf_ref[owners, j, rows, :] = part.astype(BF16).reshape(OWNERS, OWNED, DH)
+            c = pltpu.make_async_copy(buf_ref.at[pl.ds(h * OWNERS, OWNERS)], out_hbm.at[pl.ds(h * OWNERS, OWNERS)], out_sem.at[h])
+            c.start()
+            outs.append(c)
+    for c in outs:
+        c.wait()
+
+
+def dispatch(ids, q, k, v, og, w):
+    tok = pltpu.VMEM((TOK, HEADS * DH), BF16)
     return pl.pallas_call(
         dispatch_kernel,
-        grid=(HEADS // PAIR,),
-        in_specs=[pl.BlockSpec((PAIR, 1, TOK), lambda h: (h, 0, 0)), tokens, tokens, tokens],
-        out_specs=pl.BlockSpec((PAIR * OWNERS, 3, ROWS, DH), lambda h: (h, 0, 0, 0)),
-        out_shape=jax.ShapeDtypeStruct((SEQ, 3, ROWS, DH), BF16),
+        in_specs=[VM] + [ANY] * 5,
+        out_specs=ANY,
+        out_shape=jax.ShapeDtypeStruct((SEQ, 4, ROWS, DH), BF16),
+        scratch_shapes=[tok, tok, tok, pltpu.VMEM((TOK, D), BF16), pltpu.VMEM((HEADS * DH, D), BF16), pltpu.VMEM((SEQ, 4, ROWS, DH), BF16),
+            pltpu.VMEM((HEADS, MOST, CLUSTERS, TOK), BF16), pltpu.SemaphoreType.DMA((4,)), pltpu.SemaphoreType.DMA((HEADS // STEP,)), pltpu.SemaphoreType.DMA((HEADS,))],
         name="dispatch",
-    )(ids, q, k, v)
-
-
-def grad_dispatch(ids, out_grad, weight):
-    return pl.pallas_call(
-        grad_dispatch_kernel,
-        grid=(HEADS // PAIR,),
-        in_specs=[
-            pl.BlockSpec((PAIR, 1, TOK), lambda h: (h, 0, 0)),
-            pl.BlockSpec((TOK, D), lambda h: (0, 0)),
-            pl.BlockSpec((PAIR * DH, D), lambda h: (h, 0)),
-        ],
-        out_specs=pl.BlockSpec((PAIR * OWNERS, 1, ROWS, DH), lambda h: (h, 0, 0, 0)),
-        out_shape=jax.ShapeDtypeStruct((SEQ, 1, ROWS, DH), BF16),
-        name="grad_dispatch",
-    )(ids, out_grad, weight)
+    )(ids, q, k, v, og, w)
 
 
 def masks_kernel(idr_ref, idc_ref, out_ref):
@@ -173,20 +181,52 @@
     return weights * (1.0 / jnp.sum(weights, axis=0, keepdims=True))
 
 
-def forward_kernel(in_ref, q_ref, k_ref, v_ref, out_ref, o_ref):
-    regroup_in(in_ref, (q_ref, k_ref, v_ref))
-
+GROUPED = (OWNED, SLOTS, DH)
+
+
+def load_parts(in_hbm, buf, sem, js):
+    each_src = SEQ // PARTS
+    cs = []
+    for n in range(PARTS):
+        src = pl.ds(n * each_src, each_src)
+        c = pltpu.make_async_copy(in_hbm.at[src, js], buf.at[src], sem.at[n])
+        c.start(); cs.append(c)
+    return cs
+
+def forward_kernel(in_hbm, out_ref, buf_ref, q_ref, k_ref, v_ref, o_ref, sem):
+    cs = load_parts(in_hbm, buf_ref, sem, pl.ds(0, 3))
+    perm = regroup_matrix(False)
+    per = SEQ // GROUP // PARTS
+    targets = (q_ref, k_ref, v_ref)
+    for s in range(SEQ // GROUP):
+        if s % per == 0:
+            cs[s // per].wait()
+        src = slice(s * GROUP, (s + 1) * GROUP)
+        dst = slice(s * PER, (s + 1) * PER)
+        whole = jnp.concatenate([buf_ref[src, j].reshape(PB, DH) for j in range(3)], axis=1)
+        got = matmul(perm, whole).astype(BF16)
+        for j in range(3):
+            targets[j][:, dst, :] = got[:, j * DH : (j + 1) * DH].reshape(OWNED, PER, DH)
     def one(c):
         half = probabilities(q_ref[c], k_ref[c]).astype(BF16)
         o_ref[c] = matmul(half, v_ref[c], TN).astype(BF16)
-
-    each(OWNED, 2, one)
+    each(OWNED, 16, one)
     regroup_out((o_ref,), out_ref)
 
 
-def backward_kernel(in_ref, q_ref, k_ref, v_ref, out_ref, g_ref, dq_ref, dk_ref, dv_ref):
-    regroup_in(in_ref, (g_ref,))
-
+def forward(received):
+    return pl.pallas_call(
+        forward_kernel,
+        in_specs=[ANY],
+        out_specs=VM,
+        out_shape=jax.ShapeDtypeStruct((SEQ, 1, ROWS, DH), BF16),
+        scratch_shapes=[pltpu.VMEM((SEQ, 3, ROWS, DH), BF16)] + [pltpu.VMEM(GROUPED, BF16)] * 4 + [pltpu.SemaphoreType.DMA((PARTS,))],
+        name="cluster_forward",
+    )(received)
+
+
+def backward_kernel(in_ref, out_ref, q_ref, k_ref, v_ref, g_ref, dq_ref, dk_ref, dv_ref):
+    regroup_in(in_ref, (q_ref, k_ref, v_ref, g_ref))
     def one(c):
         q, k, v, g = q_ref[c], k_ref[c], v_ref[c], g_ref[c]
         probs = probabilities(q, k)
@@ -196,35 +236,19 @@
         dv_ref[c] = matmul(probs.astype(BF16), g).astype(BF16)
         dk_ref[c] = (matmul(ds, q) * SCALE).astype(BF16)
         dq_ref[c] = (matmul(ds, k, TN) * SCALE).astype(BF16)
-
-    each(OWNED, 2, one)
+    each(OWNED, 8, one)
     regroup_out((dq_ref, dk_ref, dv_ref), out_ref)
 
 
-VM = pl.BlockSpec(memory_space=pltpu.VMEM)
-GROUPED = (OWNED, SLOTS, DH)
-
-
-def forward(received):
-    return pl.pallas_call(
-        forward_kernel,
+def backward(received):
+    return pl.pallas_call(
+        backward_kernel,
         in_specs=[VM],
-        out_specs=[VM] * 4,
-        out_shape=[jax.ShapeDtypeStruct(GROUPED, BF16)] * 3 + [jax.ShapeDtypeStruct((SEQ, 1, ROWS, DH), BF16)],
-        scratch_shapes=[pltpu.VMEM(GROUPED, BF16)],
-        name="cluster_forward",
-    )(received)
-
-
-def backward(received, q, k, v):
-    return pl.pallas_call(
-        backward_kernel,
-        in_specs=[VM] * 4,
         out_specs=VM,
         out_shape=jax.ShapeDtypeStruct((SEQ, 3, ROWS, DH), BF16),
-        scratch_shapes=[pltpu.VMEM(GROUPED, BF16)] * 4,
+        scratch_shapes=[pltpu.VMEM(GROUPED, BF16)] * 7,
         name="cluster_backward",
-    )(received, q, k, v)
+    )(received)
 
 
 def attn_kernel(core_ref, mask_ref, in_ref, w_ref, attn_ref, other_ref, acc_ref):
@@ -273,27 +297,49 @@
     )(core, masks, received, weight)
 
 
-def grads_kernel(mask_ref, in_ref, dq_ref, dk_ref, dv_ref):
-    for i in range(PAIR):
-        lanes = slice(i * DH, (i + 1) * DH)
-        owners = pl.ds((pl.program_id(0) * PAIR + i) * OWNERS, OWNERS)
-        whole = jnp.concatenate([in_ref[owners, j].reshape(PER_HEAD, DH) for j in range(3)], axis=1)
-        got = matmul(mask_ref[i], whole).astype(BF16)
-        dq_ref[:, lanes] = got[:, :DH]
-        dk_ref[:, lanes] = got[:, DH : 2 * DH]
-        dv_ref[:, lanes] = got[:, 2 * DH :]
+def grads_kernel(mask_hbm, in_hbm, dq_hbm, dk_hbm, dv_hbm, mask_ref, buf_ref, out_ref, in_sem, out_sem):
+    outs = (dq_hbm, dk_hbm, dv_hbm)
+    ins = []
+    for h in range(HEADS):
+        owners = pl.ds(h * OWNERS, OWNERS)
+        a = pltpu.make_async_copy(mask_hbm.at[h], mask_ref.at[h], in_sem.at[h, 0])
+        b = pltpu.make_async_copy(in_hbm.at[owners], buf_ref.at[owners], in_sem.at[h, 1])
+        a.start()
+        b.start()
+        ins.append((a, b))
+    sent = []
+    for h in range(HEADS):
+        for c in ins[h]:
+            c.wait()
+        owners = slice(h * OWNERS, (h + 1) * OWNERS)
+        whole = jnp.concatenate([buf_ref[owners, j].reshape(PER_HEAD, DH) for j in range(3)], axis=1)
+        got = matmul(mask_ref[h], whole).astype(BF16)
+        for j in range(3):
+            out_ref[j, :, h * DH : (h + 1) * DH] = got[:, j * DH : (j + 1) * DH]
+        if h % PAIR == PAIR - 1:
+            n = h // PAIR
+            lanes = pl.ds(n * PAIR * DH, PAIR * DH)
+            for j in range(3):
+                c = pltpu.make_async_copy(out_ref.at[j, :, lanes], outs[j].at[:, lanes], out_sem.at[n, j])
+                c.start()
+                sent.append(c)
+    for c in sent:
+        c.wait()
 
 
 def grads_combine(masks, received):
     return pl.pallas_call(
         grads_kernel,
-        grid=(HEADS // PAIR,),
-        in_specs=[
-            pl.BlockSpec((PAIR, TOK, PER_HEAD), lambda h: (h, 0, 0)),
-            VM,
+        in_specs=[ANY] * 2,
+        out_specs=[ANY] * 3,
+        out_shape=[jax.ShapeDtypeStruct((TOK, HEADS * DH), BF16)] * 3,
+        scratch_shapes=[
+            pltpu.VMEM((HEADS, TOK, PER_HEAD), BF16),
+            pltpu.VMEM((SEQ, 3, ROWS, DH), BF16),
+            pltpu.VMEM((3, TOK, HEADS * DH), BF16),
+            pltpu.SemaphoreType.DMA((HEADS, 2)),
+            pltpu.SemaphoreType.DMA((HEADS // PAIR, 3)),
         ],
-        out_specs=[pl.BlockSpec((TOK, PAIR * DH), lambda h: (0, h))] * 3,
-        out_shape=[jax.ShapeDtypeStruct((TOK, HEADS * DH), BF16)] * 3,
         name="grads_combine",
     )(masks, received)
 
@@ -324,19 +370,20 @@
 
 
 def exchange(x):
-    got = lax.all_to_all(x, "seq", split_axis=0, concat_axis=0, tiled=True)
-    return pltpu.with_memory_space_constraint(got, pltpu.MemorySpace.VMEM)
+    return lax.all_to_all(x, "seq", split_axis=0, concat_axis=0, tiled=True)
+
+
+def in_vmem(x):
+    return pltpu.with_memory_space_constraint(x, pltpu.MemorySpace.VMEM)
 
 
 def body(query_rows, key_rows, value_rows, out_grad, cluster_ids, out_weight):
     idr = jnp.transpose(cluster_ids, (0, 2, 1))
     core = lax.axis_index("head").astype(jnp.int32).reshape(1)
     masks = token_masks(idr, cluster_ids)
-    received = exchange(dispatch(idr, query_rows, key_rows, value_rows))
-    grads_in = exchange(grad_dispatch(idr, out_grad, out_weight))
-    q, k, v, attn_out = forward(received)
-    attn_back = exchange(attn_out)
-    back = exchange(backward(grads_in, q, k, v))
+    received = exchange(dispatch(idr, query_rows, key_rows, value_rows, out_grad, out_weight))
+    attn_back = in_vmem(exchange(forward(received)))
+    back = exchange(backward(received))
     attn, other = attn_combine(core, masks, attn_back, out_weight)
     came = lax.ppermute(other, "head", [(0, 1), (1, 0)])
     layer_out = own_half(core, attn, out_weight, came)

time: 255 us -> 252 us (0.988)
  blocking collectives: 0 us -> 114 us
  waiting for transfers between devices: 151 us -> 67.9 us
  starting transfers between devices: 37 us -> 14.5 us
  Pallas kernels: 63.3 us -> 51.1 us
    all_to_all x0 -> x1, blocking collectives: none -> 114 us  [exchange(): return lax.all_to_all(x, 'seq', split_axis=0, concat_axis=0, tiled=True)]
    all_to_all x4 -> x2, waiting for transfers between devices: 148 us -> 65.4 us  [exchange(): return lax.all_to_all(x, 'seq', split_axis=0, concat_axis=0, tiled=True)]
    all_to_all x4 -> x2, starting transfers between devices: 37 us -> 14.5 us  [exchange(): return lax.all_to_all(x, 'seq', split_axis=0, concat_axis=0, tiled=True)]
    pallas_call x5 -> x4, Pallas kernels: 45 us -> 32.8 us  [the longest x1 12.8 us: backward(): pl.pallas_call(backward_kernel, in_specs=[VM], out_specs=VM, out_shape=ja...]
  transfers between devices with their start and end apart: 5 -> 3, of which waited for: 5 -> 3; matrix products, arithmetic and copies ran while one was open for 1% -> 1% of each run, Pallas kernels for 20% -> 12%
where the time goes in v4:
time: 252 us; the launch traced here: 251 us
  blocking collectives  114 us (45%)
  waiting for transfers between devices  67.9 us (27%)
  Pallas kernels  51.1 us (20%)
  starting transfers between devices  14.5 us (6%)
  local copies, waits for them, and re-layouts  2.55 us (1%)
    all_to_all x1, blocking collectives, exchange(): return lax.all_to_all(x, 'seq', split_axis=0, concat_axis=0, tiled=True)  114 us
    all_to_all x2, waiting for transfers between devices, exchange(): return lax.all_to_all(x, 'seq', split_axis=0, concat_axis=0, tiled=True)  65.4 us
    all_to_all x2, starting transfers between devices, exchange(): return lax.all_to_all(x, 'seq', split_axis=0, concat_axis=0, tiled=True)  14.5 us
    pallas_call x1, Pallas kernels, backward(): pl.pallas_call(backward_kernel, in_specs=[VM], out_specs=VM, out_shape=ja...  12.8 us
    pallas_call x1, Pallas kernels, dispatch(): pl.pallas_call(dispatch_kernel, in_specs=[VM] + [ANY] * 5, out_specs=ANY,...  8.48 us
    pallas_call x1, Pallas kernels, token_masks(): pl.pallas_call(masks_kernel, grid=(HEADS,), in_specs=[pl.BlockSpec((1, 1,...  7.61 us
    pallas_call x1, Pallas kernels, forward(): pl.pallas_call(forward_kernel, in_specs=[ANY], out_specs=VM, out_shape=ja...  6.37 us
    pallas_call x1, Pallas kernels, attn_combine(): pl.pallas_call(attn_kernel, grid_spec=pltpu.PrefetchScalarGridSpec(num_sc...  6.07 us
  transfers between devices with their start and end apart: 3, of which 3 were waited for; matrix products, arithmetic and copies ran while one was open for 1% of the time, Pallas kernels for 12%

profile of v4, /device:TPU:32, one launch (start us, length us, event | category | flops | bytes accessed | tf_op | source)
XLA Modules:
  0.0 250.7 jit_solution(16485355433210327839)
XLA Ops:
  0.6 8.5 %dispatch.1 = bf16[128,4,32,128]{3,2,1,0:T(8,128)(2,1)} custom-call(s32[8,1,384]{2,1,0:T(1,128)} %bitcast.2, bf16[384,1024]{1,0:T(8,128)(2,1)} %q_hbm.1, bf16[384,1024]{1,0:T(8,128)(2,1)} %k_hbm.1, bf16[384,1024]{1,0:T(8,128)(2,1)} %v_hbm.1, bf16[384,2048]{1,0:T(8,128)(2,1)} %og_hbm.1, bf16[1024,2048]{1,0:T(8,128)(2,1)} %w_ref.3), custom_call_target="tpu_custom_call" | custom-call | tf_op jit(solution)/shard_map/dispatch/pallas_call | solution.py:98
  9.1 113.9 %all_to_all.15.in_hbm.in_ref = bf16[128,4,32,128]{3,2,1,0:T(8,128)(2,1)} all-to-all(bf16[128,4,32,128]{3,2,1,0:T(8,128)(2,1)} %dispatch.1), channel_id=1, replica_groups=mesh['seq'=128,'head'=2] {'seq'}, dimensions={0} | all-to-all | bytes 8388608 | tf_op jit(solution)/shard_map/all_to_all | solution.py:373
  123.0 6.4 %cluster_forward.1 = bf16[128,1,32,128]{3,2,1,0:T(8,128)(2,1)} custom-call(bf16[128,4,32,128]{3,2,1,0:T(8,128)(2,1)} %all_to_all.15.in_hbm.in_ref), custom_call_target="tpu_custom_call" | custom-call | tf_op jit(solution)/shard_map/cluster_forward/pallas_call | solution.py:218
  129.4 6.8 %all-to-all-start.1 = ((bf16[128,1,32,128]{3,2,1,0:T(8,128)(2,1)}), bf16[128,1,32,128]{3,2,1,0:T(8,128)(2,1)S(1)}, u32[]{:S(2)}, u32[]{:S(2)}) async-start(bf16[128,1,32,128]{3,2,1,0:T(8,128)(2,1)} %cluster_forward.1), calls=%async_computation.1 | async-start | bytes 2097152 | tf_op jit(solution)/shard_map/all_to_all | solution.py:373
  136.2 12.8 %cluster_backward.1 = bf16[128,3,32,128]{3,2,1,0:T(8,128)(2,1)} custom-call(bf16[128,4,32,128]{3,2,1,0:T(8,128)(2,1)} %all_to_all.15.in_hbm.in_ref), custom_call_target="tpu_custom_call" | custom-call | tf_op jit(solution)/shard_map/cluster_backward/pallas_call | solution.py:244
  149.0 0.0 copy-start.1
  149.0 16.5 %all-to-all-done.1.in_ref = bf16[128,1,32,128]{3,2,1,0:T(8,128)(2,1)S(1)} async-done(((bf16[128,1,32,128]{3,2,1,0:T(8,128)(2,1)}), bf16[128,1,32,128]{3,2,1,0:T(8,128)(2,1)S(1)}, u32[]{:S(2)}, u32[]{:S(2)}) %all-to-all-start.1) | async-done | bytes 1048608 | tf_op jit(solution)/shard_map/all_to_all | solution.py:373
  165.5 7.7 %all-to-all-start.2 = ((bf16[128,3,32,128]{3,2,1,0:T(8,128)(2,1)}), bf16[128,3,32,128]{3,2,1,0:T(8,128)(2,1)}, u32[]{:S(2)}, u32[]{:S(2)}) async-start(bf16[128,3,32,128]{3,2,1,0:T(8,128)(2,1)} %cluster_backward.1), calls=%async_computation.2 | async-start | bytes 6291456 | tf_op jit(solution)/shard_map/all_to_all | solution.py:373
  173.2 0.0 copy-done.1
  173.2 1.7 copy.10.idc_ref
  174.9 7.6 %token_masks.1.mask_ref.mask_hbm = bf16[8,384,512]{2,1,0:T(8,128)(2,1)} custom-call(s32[8,1,384]{2,1,0:T(1,128)} %bitcast.3, s32[8,384,1]{2,1,0:T(8,128)} %copy.10.idc_ref), custom_call_target="tpu_custom_call" | custom-call | tf_op jit(solution)/shard_map/token_masks/pallas_call | solution.py:119
  182.5 6.1 %attn_combine.1 = (bf16[384,1024]{1,0:T(8,128)(2,1)}, bf16[384,1024]{1,0:T(8,128)(2,1)}) custom-call(s32[1]{0:T(128)} %bitcast.core_ref, bf16[8,384,512]{2,1,0:T(8,128)(2,1)} %token_masks.1.mask_ref.mask_hbm, bf16[128,1,32,128]{3,2,1,0:T(8,128)(2,1)S(1)} %all-to-all-done.1.in_ref, bf16[1024,2048]{1,0:T(8,128)(2,1)} %w_ref.3), custom_call_target="tpu_custom_call" | custom-call | tf_op jit(solution)/shard_map/attn_combine/pallas_call | solution.py:276
  188.5 0.0 collective-permute-start
  188.6 2.5 collective-permute-done.came_ref
  191.0 0.0 copy-start
  191.0 0.9 copy-done
  191.9 4.6 %own_half.1 = bf16[384,1024]{1,0:T(8,128)(2,1)} custom-call(s32[1]{0:T(128)} %bitcast.core_ref, bf16[384,1024]{1,0:T(8,128)(2,1)} %get-tuple-element.9.attn_ref, bf16[1024,2048]{1,0:T(8,128)(2,1)} %w_ref.3, bf16[384,1024]{1,0:T(8,128)(2,1)} %copy-done), custom_call_target="tpu_custom_call" | custom-call | tf_op jit(solution)/shard_map/own_half/pallas_call | solution.py:355
  196.5 48.9 %all-to-all-done.2.in_hbm = bf16[128,3,32,128]{3,2,1,0:T(8,128)(2,1)} async-done(((bf16[128,3,32,128]{3,2,1,0:T(8,128)(2,1)}), bf16[128,3,32,128]{3,2,1,0:T(8,128)(2,1)}, u32[]{:S(2)}, u32[]{:S(2)}) %all-to-all-start.2) | async-done | bytes 3145760 | tf_op jit(solution)/shard_map/all_to_all | solution.py:373
  245.4 5.2 %grads_combine.1 = (bf16[384,1024]{1,0:T(8,128)(2,1)}, bf16[384,1024]{1,0:T(8,128)(2,1)}, bf16[384,1024]{1,0:T(8,128)(2,1)}) custom-call(bf16[8,384,512]{2,1,0:T(8,128)(2,1)} %token_masks.1.mask_ref.mask_hbm, bf16[128,3,32,128]{3,2,1,0:T(8,128)(2,1)} %all-to-all-done.2.in_hbm), custom_call_target="tpu_custom_call" | custom-call | tf_op jit(solution)/shard_map/grads_combine/pallas_call | solution.py:331
Async XLA Ops:
  129.4 36.1 %all-to-all-start.1 = ((bf16[128,1,32,128]{3,2,1,0:T(8,128)(2,1)}), bf16[128,1,32,128]{3,2,1,0:T(8,128)(2,1)S(1)}, u32[]{:S(2)}, u32[]{:S(2)}) async-start(bf16[128,1,32,128]{3,2,1,0:T(8,128)(2,1)} %cluster_forward.1), calls=%async_computation.1 | async-start | bytes 2097152 | tf_op jit(solution)/shard_map/all_to_all | solution.py:373
  149.0 24.2 %copy-start.1 = (s32[8,384,1]{1,2,0:T(1,128)S(1)}, s32[8,384,1]{1,2,0:T(1,128)}, u32[]{:S(2)}) copy-start(s32[8,384,1]{1,2,0:T(1,128)} %param.10) | copy-start | bytes 36868
  165.5 80.0 %all-to-all-start.2 = ((bf16[128,3,32,128]{3,2,1,0:T(8,128)(2,1)}), bf16[128,3,32,128]{3,2,1,0:T(8,128)(2,1)}, u32[]{:S(2)}, u32[]{:S(2)}) async-start(bf16[128,3,32,128]{3,2,1,0:T(8,128)(2,1)} %cluster_backward.1), calls=%async_computation.2 | async-start | bytes 6291456 | tf_op jit(solution)/shard_map/all_to_all | solution.py:373
  188.5 2.5 collective-permute-start
  191.0 0.9 copy-start

commit v5 on v4

--- a/solution.py
+++ b/solution.py
@@ -21,6 +21,7 @@
 PAIR = 2
 STEP = 4
 PARTS = 4
+STAGGER_NS = 20000
 EMPTY = 64.0
 NEGATIVE = -1e30
 SCALE = DH ** -0.5
@@ -50,7 +51,7 @@
     return [jnp.where(earlier == m, hit, 0.0) for m in range(MOST)]
 
 
-def dispatch_kernel(ids_ref, q_hbm, k_hbm, v_hbm, og_hbm, w_hbm, out_hbm, q_ref, k_ref, v_ref, og_ref, w_ref, buf_ref, mask_ref, in_sem, w_sem, out_sem):
+def dispatch_kernel(core_ref, ids_ref, q_hbm, k_hbm, v_hbm, og_hbm, w_hbm, out_hbm, q_ref, k_ref, v_ref, og_ref, w_ref, buf_ref, mask_ref, in_sem, w_sem, out_sem):
     half = STEP * DH
     ins = [pltpu.make_async_copy(a, b, in_sem.at[i]) for i, (a, b) in enumerate(((og_hbm, og_ref), (q_hbm, q_ref), (k_hbm, k_ref), (v_hbm, v_ref)))]
     ws = [pltpu.make_async_copy(w_hbm.at[pl.ds(n * half, half)], w_ref.at[pl.ds(n * half, half)], w_sem.at[n]) for n in range(HEADS // STEP)]
@@ -60,6 +61,11 @@
         c.start()
     for c in ws[1:]:
         c.start()
+
+    @pl.when(core_ref[0] == 1)
+    def _():
+        pl.delay(STAGGER_NS)
+
     for h in range(HEADS):
         for m, mask in enumerate(send_masks(ids_ref[h])):
             mask_ref[h, m] = mask.astype(BF16)
@@ -93,17 +99,17 @@
         c.wait()
 
 
-def dispatch(ids, q, k, v, og, w):
+def dispatch(core, ids, q, k, v, og, w):
     tok = pltpu.VMEM((TOK, HEADS * DH), BF16)
     return pl.pallas_call(
         dispatch_kernel,
-        in_specs=[VM] + [ANY] * 5,
+        in_specs=[pl.BlockSpec(memory_space=pltpu.SMEM), VM] + [ANY] * 5,
         out_specs=ANY,
         out_shape=jax.ShapeDtypeStruct((SEQ, 4, ROWS, DH), BF16),
         scratch_shapes=[tok, tok, tok, pltpu.VMEM((TOK, D), BF16), pltpu.VMEM((HEADS * DH, D), BF16), pltpu.VMEM((SEQ, 4, ROWS, DH), BF16),
             pltpu.VMEM((HEADS, MOST, CLUSTERS, TOK), BF16), pltpu.SemaphoreType.DMA((4,)), pltpu.SemaphoreType.DMA((HEADS // STEP,)), pltpu.SemaphoreType.DMA((HEADS,))],
         name="dispatch",
-    )(ids, q, k, v, og, w)
+    )(core, ids, q, k, v, og, w)
 
 
 def masks_kernel(idr_ref, idc_ref, out_ref):
@@ -381,7 +387,7 @@
     idr = jnp.transpose(cluster_ids, (0, 2, 1))
     core = lax.axis_index("head").astype(jnp.int32).reshape(1)
     masks = token_masks(idr, cluster_ids)
-    received = exchange(dispatch(idr, query_rows, key_rows, value_rows, out_grad, out_weight))
+    received = exchange(dispatch(core, idr, query_rows, key_rows, value_rows, out_grad, out_weight))
     attn_back = in_vmem(exchange(forward(received)))
     back = exchange(backward(received))
     attn, other = attn_combine(core, masks, attn_back, out_weight)

time: 252 us -> 234 us (0.929)
  the two profiles are of different devices: /device:TPU:32 before, /device:TPU:1 now
where the time goes in v5:
time: 234 us; the launch traced here: 233 us
  blocking collectives  98.3 us (42%)
  Pallas kernels  70.2 us (30%)
  waiting for transfers between devices  47.5 us (20%)
  starting transfers between devices  13.7 us (6%)
  local copies, waits for them, and re-layouts  2.55 us (1%)
    all_to_all x1, blocking collectives, exchange(): return lax.all_to_all(x, 'seq', split_axis=0, concat_axis=0, tiled=True)  98.3 us
    all_to_all x2, waiting for transfers between devices, exchange(): return lax.all_to_all(x, 'seq', split_axis=0, concat_axis=0, tiled=True)  45 us
    pallas_call x1, Pallas kernels, dispatch(): pl.pallas_call(dispatch_kernel, in_specs=[pl.BlockSpec(memory_space=pltpu...  27.6 us
    all_to_all x2, starting transfers between devices, exchange(): return lax.all_to_all(x, 'seq', split_axis=0, concat_axis=0, tiled=True)  13.7 us
    pallas_call x1, Pallas kernels, backward(): pl.pallas_call(backward_kernel, in_specs=[VM], out_specs=VM, out_shape=ja...  12.8 us
    pallas_call x1, Pallas kernels, token_masks(): pl.pallas_call(masks_kernel, grid=(HEADS,), in_specs=[pl.BlockSpec((1, 1,...  7.61 us
    pallas_call x1, Pallas kernels, forward(): pl.pallas_call(forward_kernel, in_specs=[ANY], out_specs=VM, out_shape=ja...  6.37 us
    pallas_call x1, Pallas kernels, attn_combine(): pl.pallas_call(attn_kernel, grid_spec=pltpu.PrefetchScalarGridSpec(num_sc...  6.08 us
  transfers between devices with their start and end apart: 3, of which 3 were waited for; matrix products, arithmetic and copies ran while one was open for 1% of the time, Pallas kernels for 13%

profile of v5, /device:TPU:1, one launch (start us, length us, event | category | flops | bytes accessed | tf_op | source)
XLA Modules:
  0.0 233.1 jit_solution(14432682847202272162)
XLA Ops:
  0.6 27.6 %dispatch.1 = bf16[128,4,32,128]{3,2,1,0:T(8,128)(2,1)} custom-call(s32[1]{0:T(128)} %bitcast.core_ref, s32[8,1,384]{2,1,0:T(1,128)} %bitcast.2, bf16[384,1024]{1,0:T(8,128)(2,1)} %q_hbm.1, bf16[384,1024]{1,0:T(8,128)(2,1)} %k_hbm.1, bf16[384,1024]{1,0:T(8,128)(2,1)} %v_hbm.1, bf16[384,2048]{1,0:T(8,128)(2,1)} %og_hbm.1, bf16[1024,2048]{1,0:T(8,128)(2,1)} %w_ref.3), custom_call_target="tpu_custom_call" | custom-call | tf_op jit(solution)/shard_map/dispatch/pallas_call | solution.py:104
  28.3 98.3 %all_to_all.15.in_hbm.in_ref = bf16[128,4,32,128]{3,2,1,0:T(8,128)(2,1)} all-to-all(bf16[128,4,32,128]{3,2,1,0:T(8,128)(2,1)} %dispatch.1), channel_id=1, replica_groups=mesh['seq'=128,'head'=2] {'seq'}, dimensions={0} | all-to-all | bytes 8388608 | tf_op jit(solution)/shard_map/all_to_all | solution.py:379
  126.6 6.4 %cluster_forward.1 = bf16[128,1,32,128]{3,2,1,0:T(8,128)(2,1)} custom-call(bf16[128,4,32,128]{3,2,1,0:T(8,128)(2,1)} %all_to_all.15.in_hbm.in_ref), custom_call_target="tpu_custom_call" | custom-call | tf_op jit(solution)/shard_map/cluster_forward/pallas_call | solution.py:224
  132.9 6.4 %all-to-all-start.1 = ((bf16[128,1,32,128]{3,2,1,0:T(8,128)(2,1)}), bf16[128,1,32,128]{3,2,1,0:T(8,128)(2,1)S(1)}, u32[]{:S(2)}, u32[]{:S(2)}) async-start(bf16[128,1,32,128]{3,2,1,0:T(8,128)(2,1)} %cluster_forward.1), calls=%async_computation.1 | async-start | bytes 2097152 | tf_op jit(solution)/shard_map/all_to_all | solution.py:379
  139.3 12.8 %cluster_backward.1 = bf16[128,3,32,128]{3,2,1,0:T(8,128)(2,1)} custom-call(bf16[128,4,32,128]{3,2,1,0:T(8,128)(2,1)} %all_to_all.15.in_hbm.in_ref), custom_call_target="tpu_custom_call" | custom-call | tf_op jit(solution)/shard_map/cluster_backward/pallas_call | solution.py:250
  152.1 0.0 copy-start.1
  152.1 8.3 %all-to-all-done.1.in_ref = bf16[128,1,32,128]{3,2,1,0:T(8,128)(2,1)S(1)} async-done(((bf16[128,1,32,128]{3,2,1,0:T(8,128)(2,1)}), bf16[128,1,32,128]{3,2,1,0:T(8,128)(2,1)S(1)}, u32[]{:S(2)}, u32[]{:S(2)}) %all-to-all-start.1) | async-done | bytes 1048608 | tf_op jit(solution)/shard_map/all_to_all | solution.py:379
  160.4 7.3 %all-to-all-start.2 = ((bf16[128,3,32,128]{3,2,1,0:T(8,128)(2,1)}), bf16[128,3,32,128]{3,2,1,0:T(8,128)(2,1)}, u32[]{:S(2)}, u32[]{:S(2)}) async-start(bf16[128,3,32,128]{3,2,1,0:T(8,128)(2,1)} %cluster_backward.1), calls=%async_computation.2 | async-start | bytes 6291456 | tf_op jit(solution)/shard_map/all_to_all | solution.py:379
  167.7 0.0 copy-done.1
  167.7 1.7 copy.10.idc_ref
  169.4 7.6 %token_masks.1.mask_ref.mask_hbm = bf16[8,384,512]{2,1,0:T(8,128)(2,1)} custom-call(s32[8,1,384]{2,1,0:T(1,128)} %bitcast.3, s32[8,384,1]{2,1,0:T(8,128)} %copy.10.idc_ref), custom_call_target="tpu_custom_call" | custom-call | tf_op jit(solution)/shard_map/token_masks/pallas_call | solution.py:125
  177.0 6.1 %attn_combine.1 = (bf16[384,1024]{1,0:T(8,128)(2,1)}, bf16[384,1024]{1,0:T(8,128)(2,1)}) custom-call(s32[1]{0:T(128)} %bitcast.core_ref, bf16[8,384,512]{2,1,0:T(8,128)(2,1)} %token_masks.1.mask_ref.mask_hbm, bf16[128,1,32,128]{3,2,1,0:T(8,128)(2,1)S(1)} %all-to-all-done.1.in_ref, bf16[1024,2048]{1,0:T(8,128)(2,1)} %w_ref.3), custom_call_target="tpu_custom_call" | custom-call | tf_op jit(solution)/shard_map/attn_combine/pallas_call | solution.py:282
  183.1 0.0 collective-permute-start
  183.1 2.5 %collective-permute-done.came_ref = bf16[384,1024]{1,0:T(8,128)(2,1)S(1)} collective-permute-done((bf16[384,1024]{1,0:T(8,128)(2,1)}, bf16[384,1024]{1,0:T(8,128)(2,1)S(1)}, u32[]{:S(2)}, u32[]{:S(2)}) %collective-permute-start) | collective-permute-done | bytes 786464 | tf_op jit(solution)/shard_map/ppermute | solution.py:394
  185.6 0.0 copy-start
  185.6 0.9 copy-done
  186.4 4.6 %own_half.1 = bf16[384,1024]{1,0:T(8,128)(2,1)} custom-call(s32[1]{0:T(128)} %bitcast.core_ref, bf16[384,1024]{1,0:T(8,128)(2,1)} %get-tuple-element.9.attn_ref, bf16[1024,2048]{1,0:T(8,128)(2,1)} %w_ref.3, bf16[384,1024]{1,0:T(8,128)(2,1)} %copy-done), custom_call_target="tpu_custom_call" | custom-call | tf_op jit(solution)/shard_map/own_half/pallas_call | solution.py:361
  191.1 36.8 %all-to-all-done.2.in_hbm = bf16[128,3,32,128]{3,2,1,0:T(8,128)(2,1)} async-done(((bf16[128,3,32,128]{3,2,1,0:T(8,128)(2,1)}), bf16[128,3,32,128]{3,2,1,0:T(8,128)(2,1)}, u32[]{:S(2)}, u32[]{:S(2)}) %all-to-all-start.2) | async-done | bytes 3145760 | tf_op jit(solution)/shard_map/all_to_all | solution.py:379
  227.8 5.2 %grads_combine.1 = (bf16[384,1024]{1,0:T(8,128)(2,1)}, bf16[384,1024]{1,0:T(8,128)(2,1)}, bf16[384,1024]{1,0:T(8,128)(2,1)}) custom-call(bf16[8,384,512]{2,1,0:T(8,128)(2,1)} %token_masks.1.mask_ref.mask_hbm, bf16[128,3,32,128]{3,2,1,0:T(8,128)(2,1)} %all-to-all-done.2.in_hbm), custom_call_target="tpu_custom_call" | custom-call | tf_op jit(solution)/shard_map/grads_combine/pallas_call | solution.py:337
Async XLA Ops:
  132.9 27.4 %all-to-all-start.1 = ((bf16[128,1,32,128]{3,2,1,0:T(8,128)(2,1)}), bf16[128,1,32,128]{3,2,1,0:T(8,128)(2,1)S(1)}, u32[]{:S(2)}, u32[]{:S(2)}) async-start(bf16[128,1,32,128]{3,2,1,0:T(8,128)(2,1)} %cluster_forward.1), calls=%async_computation.1 | async-start | bytes 2097152 | tf_op jit(solution)/shard_map/all_to_all | solution.py:379
  152.1 15.6 %copy-start.1 = (s32[8,384,1]{1,2,0:T(1,128)S(1)}, s32[8,384,1]{1,2,0:T(1,128)}, u32[]{:S(2)}) copy-start(s32[8,384,1]{1,2,0:T(1,128)} %param.10) | copy-start | bytes 36868
  160.4 67.5 %all-to-all-start.2 = ((bf16[128,3,32,128]{3,2,1,0:T(8,128)(2,1)}), bf16[128,3,32,128]{3,2,1,0:T(8,128)(2,1)}, u32[]{:S(2)}, u32[]{:S(2)}) async-start(bf16[128,3,32,128]{3,2,1,0:T(8,128)(2,1)} %cluster_backward.1), calls=%async_computation.2 | async-start | bytes 6291456 | tf_op jit(solution)/shard_map/all_to_all | solution.py:379
  183.1 2.5 %collective-permute-start = (bf16[384,1024]{1,0:T(8,128)(2,1)}, bf16[384,1024]{1,0:T(8,128)(2,1)S(1)}, u32[]{:S(2)}, u32[]{:S(2)}) collective-permute-start(bf16[384,1024]{1,0:T(8,128)(2,1)} %get-tuple-element.10), channel_id=1, source_target_pairs={{0,1},{1,0},{2,3},{3,2},{4,5},{5,4},{6,7},{7,6},{8,9},{9,8},{10,11... | collective-permute-start | bytes 2359304 | tf_op jit(solution)/shard_map/ppermute | solution.py:394
  185.6 0.9 copy-start

commit v6 on v5

--- a/solution.py
+++ b/solution.py
@@ -20,8 +20,7 @@
 GROUP = 8
 PAIR = 2
 STEP = 4
-PARTS = 4
-STAGGER_NS = 20000
+STAGGER_NS = 45000
 EMPTY = 64.0
 NEGATIVE = -1e30
 SCALE = DH ** -0.5
@@ -190,78 +189,40 @@
 GROUPED = (OWNED, SLOTS, DH)
 
 
-def load_parts(in_hbm, buf, sem, js):
-    each_src = SEQ // PARTS
-    cs = []
-    for n in range(PARTS):
-        src = pl.ds(n * each_src, each_src)
-        c = pltpu.make_async_copy(in_hbm.at[src, js], buf.at[src], sem.at[n])
-        c.start(); cs.append(c)
-    return cs
-
-def forward_kernel(in_hbm, out_ref, buf_ref, q_ref, k_ref, v_ref, o_ref, sem):
-    cs = load_parts(in_hbm, buf_ref, sem, pl.ds(0, 3))
-    perm = regroup_matrix(False)
-    per = SEQ // GROUP // PARTS
-    targets = (q_ref, k_ref, v_ref)
-    for s in range(SEQ // GROUP):
-        if s % per == 0:
-            cs[s // per].wait()
-        src = slice(s * GROUP, (s + 1) * GROUP)
-        dst = slice(s * PER, (s + 1) * PER)
-        whole = jnp.concatenate([buf_ref[src, j].reshape(PB, DH) for j in range(3)], axis=1)
-        got = matmul(perm, whole).astype(BF16)
-        for j in range(3):
-            targets[j][:, dst, :] = got[:, j * DH : (j + 1) * DH].reshape(OWNED, PER, DH)
-    def one(c):
-        half = probabilities(q_ref[c], k_ref[c]).astype(BF16)
-        o_ref[c] = matmul(half, v_ref[c], TN).astype(BF16)
-    each(OWNED, 16, one)
-    regroup_out((o_ref,), out_ref)
-
-
-def forward(received):
-    return pl.pallas_call(
-        forward_kernel,
-        in_specs=[ANY],
-        out_specs=VM,
-        out_shape=jax.ShapeDtypeStruct((SEQ, 1, ROWS, DH), BF16),
-        scratch_shapes=[pltpu.VMEM((SEQ, 3, ROWS, DH), BF16)] + [pltpu.VMEM(GROUPED, BF16)] * 4 + [pltpu.SemaphoreType.DMA((PARTS,))],
-        name="cluster_forward",
-    )(received)
-
-
-def backward_kernel(in_ref, out_ref, q_ref, k_ref, v_ref, g_ref, dq_ref, dk_ref, dv_ref):
+def owner_kernel(in_ref, out_ref, q_ref, k_ref, v_ref, g_ref, o_ref, dq_ref, dk_ref, dv_ref):
     regroup_in(in_ref, (q_ref, k_ref, v_ref, g_ref))
+
     def one(c):
         q, k, v, g = q_ref[c], k_ref[c], v_ref[c], g_ref[c]
         probs = probabilities(q, k)
+        half = probs.astype(BF16)
         dprob = matmul(v, g, NT)
         delta = jnp.sum(probs * dprob, axis=0, keepdims=True)
         ds = (probs * (dprob - delta)).astype(BF16)
-        dv_ref[c] = matmul(probs.astype(BF16), g).astype(BF16)
+        o_ref[c] = matmul(half, v, TN).astype(BF16)
+        dv_ref[c] = matmul(half, g).astype(BF16)
         dk_ref[c] = (matmul(ds, q) * SCALE).astype(BF16)
         dq_ref[c] = (matmul(ds, k, TN) * SCALE).astype(BF16)
+
     each(OWNED, 8, one)
-    regroup_out((dq_ref, dk_ref, dv_ref), out_ref)
-
-
-def backward(received):
-    return pl.pallas_call(
-        backward_kernel,
+    regroup_out((o_ref, dq_ref, dk_ref, dv_ref), out_ref)
+
+
+def owner(received):
+    return pl.pallas_call(
+        owner_kernel,
         in_specs=[VM],
         out_specs=VM,
-        out_shape=jax.ShapeDtypeStruct((SEQ, 3, ROWS, DH), BF16),
-        scratch_shapes=[pltpu.VMEM(GROUPED, BF16)] * 7,
-        name="cluster_backward",
+        out_shape=jax.ShapeDtypeStruct((SEQ, 4, ROWS, DH), BF16),
+        scratch_shapes=[pltpu.VMEM(GROUPED, BF16)] * 8,
+        name="owner",
     )(received)
 
 
 def attn_kernel(core_ref, mask_ref, in_ref, w_ref, attn_ref, other_ref, acc_ref):
     h = pl.program_id(0)
     for i in range(PAIR):
-        owners = pl.ds((h * PAIR + i) * OWNERS, OWNERS)
-        rows = in_ref[owners, 0].reshape(PER_HEAD, DH)
+        rows = in_ref[i * OWNERS : (i + 1) * OWNERS, 0].reshape(PER_HEAD, DH)
         attn_ref[:, i * DH : (i + 1) * DH] = matmul(mask_ref[i], rows).astype(BF16)
     part = matmul(attn_ref[...], w_ref[...])
 
@@ -286,7 +247,7 @@
             grid=(HEADS // PAIR,),
             in_specs=[
                 pl.BlockSpec((PAIR, TOK, PER_HEAD), lambda h, core: (h, 0, 0)),
-                VM,
+                pl.BlockSpec((PAIR * OWNERS, 1, ROWS, DH), lambda h, core: (h, 0, 0, 0)),
                 pl.BlockSpec((PAIR * DH, D // 2), lambda h, core: (h, 1 - core[0])),
             ],
             out_specs=[
@@ -309,7 +270,7 @@
     for h in range(HEADS):
         owners = pl.ds(h * OWNERS, OWNERS)
         a = pltpu.make_async_copy(mask_hbm.at[h], mask_ref.at[h], in_sem.at[h, 0])
-        b = pltpu.make_async_copy(in_hbm.at[owners], buf_ref.at[owners], in_sem.at[h, 1])
+        b = pltpu.make_async_copy(in_hbm.at[owners, pl.ds(1, 3)], buf_ref.at[owners], in_sem.at[h, 1])
         a.start()
         b.start()
         ins.append((a, b))
@@ -379,18 +340,13 @@
     return lax.all_to_all(x, "seq", split_axis=0, concat_axis=0, tiled=True)
 
 
-def in_vmem(x):
-    return pltpu.with_memory_space_constraint(x, pltpu.MemorySpace.VMEM)
-
-
 def body(query_rows, key_rows, value_rows, out_grad, cluster_ids, out_weight):
     idr = jnp.transpose(cluster_ids, (0, 2, 1))
     core = lax.axis_index("head").astype(jnp.int32).reshape(1)
     masks = token_masks(idr, cluster_ids)
     received = exchange(dispatch(core, idr, query_rows, key_rows, value_rows, out_grad, out_weight))
-    attn_back = in_vmem(exchange(forward(received)))
-    back = exchange(backward(received))
-    attn, other = attn_combine(core, masks, attn_back, out_weight)
+    back = exchange(owner(received))
+    attn, other = attn_combine(core, masks, back, out_weight)
     came = lax.ppermute(other, "head", [(0, 1), (1, 0)])
     layer_out = own_half(core, attn, out_weight, came)
     dq, dk, dv = grads_combine(masks, back)

time: 234 us -> 234 us (level)
  the two profiles are of different devices: /device:TPU:1 before, /device:TPU:32 now
where the time goes in v6:
time: 234 us; the launch traced here: 231 us
  blocking collectives  72.9 us (31%)
  waiting for transfers between devices  60.3 us (26%)
  starting transfers between devices  48.6 us (21%)
  Pallas kernels  46 us (20%)
  local copies, waits for them, and re-layouts  2.59 us (1%)
    all_to_all x1, blocking collectives, exchange(): return lax.all_to_all(x, 'seq', split_axis=0, concat_axis=0, tiled=True)  72.9 us
    all_to_all x1, waiting for transfers between devices, exchange(): return lax.all_to_all(x, 'seq', split_axis=0, concat_axis=0, tiled=True)  60.3 us
    ppermute x1, starting transfers between devices, body(): came = lax.ppermute(other, 'head', [(0, 1), (1, 0)])  41.9 us
    pallas_call x1, Pallas kernels, owner(): pl.pallas_call(owner_kernel, in_specs=[VM], out_specs=VM, out_shape=jax.S...  13.8 us
    pallas_call x1, Pallas kernels, dispatch(): pl.pallas_call(dispatch_kernel, in_specs=[pl.BlockSpec(memory_space=pltpu...  8.53 us
    pallas_call x1, Pallas kernels, token_masks(): pl.pallas_call(masks_kernel, grid=(HEADS,), in_specs=[pl.BlockSpec((1, 1,...  7.64 us
    all_to_all x1, starting transfers between devices, exchange(): return lax.all_to_all(x, 'seq', split_axis=0, concat_axis=0, tiled=True)  6.65 us
    pallas_call x1, Pallas kernels, attn_combine(): pl.pallas_call(attn_kernel, grid_spec=pltpu.PrefetchScalarGridSpec(num_sc...  6.26 us
  transfers between devices with their start and end apart: 2, of which 1 were waited for; matrix products, arithmetic and copies ran while one was open for 1% of the time, Pallas kernels for 6%

profile of v6, /device:TPU:32, one launch (start us, length us, event | category | flops | bytes accessed | tf_op | source)
XLA Modules:
  0.0 231.1 jit_solution(9740270810742567727)
XLA Ops:
  0.6 8.5 %dispatch.1 = bf16[128,4,32,128]{3,2,1,0:T(8,128)(2,1)} custom-call(s32[1]{0:T(128)} %bitcast.core_ref, s32[8,1,384]{2,1,0:T(1,128)} %bitcast.2, bf16[384,1024]{1,0:T(8,128)(2,1)} %q_hbm.1, bf16[384,1024]{1,0:T(8,128)(2,1)} %k_hbm.1, bf16[384,1024]{1,0:T(8,128)(2,1)} %v_hbm.1, bf16[384,2048]{1,0:T(8,128)(2,1)} %og_hbm.1, bf16[1024,2048]{1,0:T(8,128)(2,1)} %w_ref.3), custom_call_target="tpu_custom_call" | custom-call | tf_op jit(solution)/shard_map/dispatch/pallas_call | solution.py:103
  9.2 72.9 %all_to_all.10.in_ref = bf16[128,4,32,128]{3,2,1,0:T(8,128)(2,1)} all-to-all(bf16[128,4,32,128]{3,2,1,0:T(8,128)(2,1)} %dispatch.1), channel_id=1, replica_groups=mesh['seq'=128,'head'=2] {'seq'}, dimensions={0} | all-to-all | bytes 8388608 | tf_op jit(solution)/shard_map/all_to_all | solution.py:340
  82.1 13.8 %owner.1 = bf16[128,4,32,128]{3,2,1,0:T(8,128)(2,1)} custom-call(bf16[128,4,32,128]{3,2,1,0:T(8,128)(2,1)} %all_to_all.10.in_ref), custom_call_target="tpu_custom_call" | custom-call | tf_op jit(solution)/shard_map/owner/pallas_call | solution.py:212
  95.9 0.0 copy-start.1
  95.9 6.6 %all-to-all-start.1 = ((bf16[128,4,32,128]{3,2,1,0:T(8,128)(2,1)}), bf16[128,4,32,128]{3,2,1,0:T(8,128)(2,1)}, u32[]{:S(2)}, u32[]{:S(2)}) async-start(bf16[128,4,32,128]{3,2,1,0:T(8,128)(2,1)} %owner.1), calls=%async_computation.1 | async-start | bytes 8388608 | tf_op jit(solution)/shard_map/all_to_all | solution.py:340
  102.6 0.0 copy-done.1
  102.6 1.7 copy.10.idc_ref
  104.3 7.6 %token_masks.1.mask_ref.mask_hbm = bf16[8,384,512]{2,1,0:T(8,128)(2,1)} custom-call(s32[8,1,384]{2,1,0:T(1,128)} %bitcast.3, s32[8,384,1]{2,1,0:T(8,128)} %copy.10.idc_ref), custom_call_target="tpu_custom_call" | custom-call | tf_op jit(solution)/shard_map/token_masks/pallas_call | solution.py:124
  111.9 60.3 %all-to-all-done.1.in_ref.in_hbm = bf16[128,4,32,128]{3,2,1,0:T(8,128)(2,1)} async-done(((bf16[128,4,32,128]{3,2,1,0:T(8,128)(2,1)}), bf16[128,4,32,128]{3,2,1,0:T(8,128)(2,1)}, u32[]{:S(2)}, u32[]{:S(2)}) %all-to-all-start.1) | async-done | bytes 4194336 | tf_op jit(solution)/shard_map/all_to_all | solution.py:340
  172.2 6.3 %attn_combine.1 = (bf16[384,1024]{1,0:T(8,128)(2,1)}, bf16[384,1024]{1,0:T(8,128)(2,1)}) custom-call(s32[1]{0:T(128)} %bitcast.core_ref, bf16[8,384,512]{2,1,0:T(8,128)(2,1)} %token_masks.1.mask_ref.mask_hbm, bf16[128,4,32,128]{3,2,1,0:T(8,128)(2,1)} %all-to-all-done.1.in_ref.in_hbm, bf16[1024,2048]{1,0:T(8,128)(2,1)} %w_ref.3), custom_call_target="tpu_custom_call" | custom-call | tf_op jit(solution)/shard_map/attn_combine/pallas_call | solution.py:243
  178.5 41.9 %collective-permute-start = (bf16[384,1024]{1,0:T(8,128)(2,1)}, bf16[384,1024]{1,0:T(8,128)(2,1)S(1)}, u32[]{:S(2)}, u32[]{:S(2)}) collective-permute-start(bf16[384,1024]{1,0:T(8,128)(2,1)} %get-tuple-element.10), channel_id=1, source_target_pairs={{0,1},{1,0},{2,3},{3,2},{4,5},{5,4},{6,7},{7,6},{8,9},{9,8},{10,11... | collective-permute-start | bytes 2359304 | tf_op jit(solution)/shard_map/ppermute | solution.py:350
  220.4 5.2 %grads_combine.1 = (bf16[384,1024]{1,0:T(8,128)(2,1)}, bf16[384,1024]{1,0:T(8,128)(2,1)}, bf16[384,1024]{1,0:T(8,128)(2,1)}) custom-call(bf16[8,384,512]{2,1,0:T(8,128)(2,1)} %token_masks.1.mask_ref.mask_hbm, bf16[128,4,32,128]{3,2,1,0:T(8,128)(2,1)} %all-to-all-done.1.in_ref.in_hbm), custom_call_target="tpu_custom_call" | custom-call | tf_op jit(solution)/shard_map/grads_combine/pallas_call | solution.py:298
  225.6 0.0 collective-permute-done.came_ref
  225.6 0.0 copy-start
  225.6 0.9 copy-done
  226.5 4.6 %own_half.1 = bf16[384,1024]{1,0:T(8,128)(2,1)} custom-call(s32[1]{0:T(128)} %bitcast.core_ref, bf16[384,1024]{1,0:T(8,128)(2,1)} %get-tuple-element.9.attn_ref, bf16[1024,2048]{1,0:T(8,128)(2,1)} %w_ref.3, bf16[384,1024]{1,0:T(8,128)(2,1)} %copy-done), custom_call_target="tpu_custom_call" | custom-call | tf_op jit(solution)/shard_map/own_half/pallas_call | solution.py:322
Async XLA Ops:
  95.9 6.7 %copy-start.1 = (s32[8,384,1]{1,2,0:T(1,128)S(1)}, s32[8,384,1]{1,2,0:T(1,128)}, u32[]{:S(2)}) copy-start(s32[8,384,1]{1,2,0:T(1,128)} %param.10) | copy-start | bytes 36868
  95.9 76.3 %all-to-all-start.1 = ((bf16[128,4,32,128]{3,2,1,0:T(8,128)(2,1)}), bf16[128,4,32,128]{3,2,1,0:T(8,128)(2,1)}, u32[]{:S(2)}, u32[]{:S(2)}) async-start(bf16[128,4,32,128]{3,2,1,0:T(8,128)(2,1)} %owner.1), calls=%async_computation.1 | async-start | bytes 8388608 | tf_op jit(solution)/shard_map/all_to_all | solution.py:340
  178.5 47.1 %collective-permute-start = (bf16[384,1024]{1,0:T(8,128)(2,1)}, bf16[384,1024]{1,0:T(8,128)(2,1)S(1)}, u32[]{:S(2)}, u32[]{:S(2)}) collective-permute-start(bf16[384,1024]{1,0:T(8,128)(2,1)} %get-tuple-element.10), channel_id=1, source_target_pairs={{0,1},{1,0},{2,3},{3,2},{4,5},{5,4},{6,7},{7,6},{8,9},{9,8},{10,11... | collective-permute-start | bytes 2359304 | tf_op jit(solution)/shard_map/ppermute | solution.py:350
  225.6 0.9 copy-start

commit v7 on v5

--- a/solution.py
+++ b/solution.py
@@ -21,7 +21,7 @@
 PAIR = 2
 STEP = 4
 PARTS = 4
-STAGGER_NS = 20000
+STAGGER_NS = 28000
 EMPTY = 64.0
 NEGATIVE = -1e30
 SCALE = DH ** -0.5

time: 234 us -> 236 us (level)
  Pallas kernels: 70.2 us -> 78.2 us
  blocking collectives: 98.3 us -> 92.1 us
    pallas_call x1, Pallas kernels: 27.6 us -> 35.6 us  [dispatch(): pl.pallas_call(dispatch_kernel, in_specs=[pl.BlockSpec(memory_space=pltpu...]
    all_to_all x1, blocking collectives: 98.3 us -> 92.1 us  [exchange(): return lax.all_to_all(x, 'seq', split_axis=0, concat_axis=0, tiled=True)]
where the time goes in v7:
time: 236 us
  blocking collectives  92.1 us (39%)
  Pallas kernels  78.2 us (33%)
  waiting for transfers between devices  47.5 us (20%)
  starting transfers between devices  14.3 us (6%)
  local copies, waits for them, and re-layouts  2.55 us (1%)
    all_to_all x1, blocking collectives, exchange(): return lax.all_to_all(x, 'seq', split_axis=0, concat_axis=0, tiled=True)  92.1 us
    all_to_all x2, waiting for transfers between devices, exchange(): return lax.all_to_all(x, 'seq', split_axis=0, concat_axis=0, tiled=True)  45 us
    pallas_call x1, Pallas kernels, dispatch(): pl.pallas_call(dispatch_kernel, in_specs=[pl.BlockSpec(memory_space=pltpu...  35.6 us
    all_to_all x2, starting transfers between devices, exchange(): return lax.all_to_all(x, 'seq', split_axis=0, concat_axis=0, tiled=True)  14.3 us
    pallas_call x1, Pallas kernels, backward(): pl.pallas_call(backward_kernel, in_specs=[VM], out_specs=VM, out_shape=ja...  12.8 us
    pallas_call x1, Pallas kernels, token_masks(): pl.pallas_call(masks_kernel, grid=(HEADS,), in_specs=[pl.BlockSpec((1, 1,...  7.61 us
    pallas_call x1, Pallas kernels, forward(): pl.pallas_call(forward_kernel, in_specs=[ANY], out_specs=VM, out_shape=ja...  6.37 us
    pallas_call x1, Pallas kernels, attn_combine(): pl.pallas_call(attn_kernel, grid_spec=pltpu.PrefetchScalarGridSpec(num_sc...  6.08 us
  transfers between devices with their start and end apart: 3, of which 3 were waited for; matrix products, arithmetic and copies ran while one was open for 1% of the time, Pallas kernels for 13%

profile of v7, /device:TPU:1, one launch (start us, length us, event | category | flops | bytes accessed | tf_op | source)
XLA Modules:
  0.0 235.6 jit_solution(15187111735961310726)
XLA Ops:
  0.6 35.6 %dispatch.1 = bf16[128,4,32,128]{3,2,1,0:T(8,128)(2,1)} custom-call(s32[1]{0:T(128)} %bitcast.core_ref, s32[8,1,384]{2,1,0:T(1,128)} %bitcast.2, bf16[384,1024]{1,0:T(8,128)(2,1)} %q_hbm.1, bf16[384,1024]{1,0:T(8,128)(2,1)} %k_hbm.1, bf16[384,1024]{1,0:T(8,128)(2,1)} %v_hbm.1, bf16[384,2048]{1,0:T(8,128)(2,1)} %og_hbm.1, bf16[1024,2048]{1,0:T(8,128)(2,1)} %w_ref.3), custom_call_target="tpu_custom_call" | custom-call | tf_op jit(solution)/shard_map/dispatch/pallas_call | solution.py:104
  36.3 92.1 %all_to_all.15.in_hbm.in_ref = bf16[128,4,32,128]{3,2,1,0:T(8,128)(2,1)} all-to-all(bf16[128,4,32,128]{3,2,1,0:T(8,128)(2,1)} %dispatch.1), channel_id=1, replica_groups=mesh['seq'=128,'head'=2] {'seq'}, dimensions={0} | all-to-all | bytes 8388608 | tf_op jit(solution)/shard_map/all_to_all | solution.py:379
  128.4 6.4 %cluster_forward.1 = bf16[128,1,32,128]{3,2,1,0:T(8,128)(2,1)} custom-call(bf16[128,4,32,128]{3,2,1,0:T(8,128)(2,1)} %all_to_all.15.in_hbm.in_ref), custom_call_target="tpu_custom_call" | custom-call | tf_op jit(solution)/shard_map/cluster_forward/pallas_call | solution.py:224
  134.8 7.0 %all-to-all-start.1 = ((bf16[128,1,32,128]{3,2,1,0:T(8,128)(2,1)}), bf16[128,1,32,128]{3,2,1,0:T(8,128)(2,1)S(1)}, u32[]{:S(2)}, u32[]{:S(2)}) async-start(bf16[128,1,32,128]{3,2,1,0:T(8,128)(2,1)} %cluster_forward.1), calls=%async_computation.1 | async-start | bytes 2097152 | tf_op jit(solution)/shard_map/all_to_all | solution.py:379
  141.8 12.8 %cluster_backward.1 = bf16[128,3,32,128]{3,2,1,0:T(8,128)(2,1)} custom-call(bf16[128,4,32,128]{3,2,1,0:T(8,128)(2,1)} %all_to_all.15.in_hbm.in_ref), custom_call_target="tpu_custom_call" | custom-call | tf_op jit(solution)/shard_map/cluster_backward/pallas_call | solution.py:250
  154.5 0.0 copy-start.1
  154.5 15.0 %all-to-all-done.1.in_ref = bf16[128,1,32,128]{3,2,1,0:T(8,128)(2,1)S(1)} async-done(((bf16[128,1,32,128]{3,2,1,0:T(8,128)(2,1)}), bf16[128,1,32,128]{3,2,1,0:T(8,128)(2,1)S(1)}, u32[]{:S(2)}, u32[]{:S(2)}) %all-to-all-start.1) | async-done | bytes 1048608 | tf_op jit(solution)/shard_map/all_to_all | solution.py:379
  169.6 7.3 %all-to-all-start.2 = ((bf16[128,3,32,128]{3,2,1,0:T(8,128)(2,1)}), bf16[128,3,32,128]{3,2,1,0:T(8,128)(2,1)}, u32[]{:S(2)}, u32[]{:S(2)}) async-start(bf16[128,3,32,128]{3,2,1,0:T(8,128)(2,1)} %cluster_backward.1), calls=%async_computation.2 | async-start | bytes 6291456 | tf_op jit(solution)/shard_map/all_to_all | solution.py:379
  176.9 0.0 copy-done.1
  176.9 1.7 copy.10.idc_ref
  178.6 7.6 %token_masks.1.mask_ref.mask_hbm = bf16[8,384,512]{2,1,0:T(8,128)(2,1)} custom-call(s32[8,1,384]{2,1,0:T(1,128)} %bitcast.3, s32[8,384,1]{2,1,0:T(8,128)} %copy.10.idc_ref), custom_call_target="tpu_custom_call" | custom-call | tf_op jit(solution)/shard_map/token_masks/pallas_call | solution.py:125
  186.2 6.1 %attn_combine.1 = (bf16[384,1024]{1,0:T(8,128)(2,1)}, bf16[384,1024]{1,0:T(8,128)(2,1)}) custom-call(s32[1]{0:T(128)} %bitcast.core_ref, bf16[8,384,512]{2,1,0:T(8,128)(2,1)} %token_masks.1.mask_ref.mask_hbm, bf16[128,1,32,128]{3,2,1,0:T(8,128)(2,1)S(1)} %all-to-all-done.1.in_ref, bf16[1024,2048]{1,0:T(8,128)(2,1)} %w_ref.3), custom_call_target="tpu_custom_call" | custom-call | tf_op jit(solution)/shard_map/attn_combine/pallas_call | solution.py:282
  192.3 0.0 collective-permute-start
  192.3 2.5 %collective-permute-done.came_ref = bf16[384,1024]{1,0:T(8,128)(2,1)S(1)} collective-permute-done((bf16[384,1024]{1,0:T(8,128)(2,1)}, bf16[384,1024]{1,0:T(8,128)(2,1)S(1)}, u32[]{:S(2)}, u32[]{:S(2)}) %collective-permute-start) | collective-permute-done | bytes 786464 | tf_op jit(solution)/shard_map/ppermute | solution.py:394
  194.8 0.0 copy-start
  194.8 0.9 copy-done
  195.6 4.6 %own_half.1 = bf16[384,1024]{1,0:T(8,128)(2,1)} custom-call(s32[1]{0:T(128)} %bitcast.core_ref, bf16[384,1024]{1,0:T(8,128)(2,1)} %get-tuple-element.9.attn_ref, bf16[1024,2048]{1,0:T(8,128)(2,1)} %w_ref.3, bf16[384,1024]{1,0:T(8,128)(2,1)} %copy-done), custom_call_target="tpu_custom_call" | custom-call | tf_op jit(solution)/shard_map/own_half/pallas_call | solution.py:361
  200.2 30.0 %all-to-all-done.2.in_hbm = bf16[128,3,32,128]{3,2,1,0:T(8,128)(2,1)} async-done(((bf16[128,3,32,128]{3,2,1,0:T(8,128)(2,1)}), bf16[128,3,32,128]{3,2,1,0:T(8,128)(2,1)}, u32[]{:S(2)}, u32[]{:S(2)}) %all-to-all-start.2) | async-done | bytes 3145760 | tf_op jit(solution)/shard_map/all_to_all | solution.py:379
  230.2 5.2 %grads_combine.1 = (bf16[384,1024]{1,0:T(8,128)(2,1)}, bf16[384,1024]{1,0:T(8,128)(2,1)}, bf16[384,1024]{1,0:T(8,128)(2,1)}) custom-call(bf16[8,384,512]{2,1,0:T(8,128)(2,1)} %token_masks.1.mask_ref.mask_hbm, bf16[128,3,32,128]{3,2,1,0:T(8,128)(2,1)} %all-to-all-done.2.in_hbm), custom_call_target="tpu_custom_call" | custom-call | tf_op jit(solution)/shard_map/grads_combine/pallas_call | solution.py:337
Async XLA Ops:
  134.8 34.8 %all-to-all-start.1 = ((bf16[128,1,32,128]{3,2,1,0:T(8,128)(2,1)}), bf16[128,1,32,128]{3,2,1,0:T(8,128)(2,1)S(1)}, u32[]{:S(2)}, u32[]{:S(2)}) async-start(bf16[128,1,32,128]{3,2,1,0:T(8,128)(2,1)} %cluster_forward.1), calls=%async_computation.1 | async-start | bytes 2097152 | tf_op jit(solution)/shard_map/all_to_all | solution.py:379
  154.5 22.3 %copy-start.1 = (s32[8,384,1]{1,2,0:T(1,128)S(1)}, s32[8,384,1]{1,2,0:T(1,128)}, u32[]{:S(2)}) copy-start(s32[8,384,1]{1,2,0:T(1,128)} %param.10) | copy-start | bytes 36868
  169.6 60.7 %all-to-all-start.2 = ((bf16[128,3,32,128]{3,2,1,0:T(8,128)(2,1)}), bf16[128,3,32,128]{3,2,1,0:T(8,128)(2,1)}, u32[]{:S(2)}, u32[]{:S(2)}) async-start(bf16[128,3,32,128]{3,2,1,0:T(8,128)(2,1)} %cluster_backward.1), calls=%async_computation.2 | async-start | bytes 6291456 | tf_op jit(solution)/shard_map/all_to_all | solution.py:379
  192.3 2.5 %collective-permute-start = (bf16[384,1024]{1,0:T(8,128)(2,1)}, bf16[384,1024]{1,0:T(8,128)(2,1)S(1)}, u32[]{:S(2)}, u32[]{:S(2)}) collective-permute-start(bf16[384,1024]{1,0:T(8,128)(2,1)} %get-tuple-element.10), channel_id=1, source_target_pairs={{0,1},{1,0},{2,3},{3,2},{4,5},{5,4},{6,7},{7,6},{8,9},{9,8},{10,11... | collective-permute-start | bytes 2359304 | tf_op jit(solution)/shard_map/ppermute | solution.py:394
  194.8 0.9 copy-start
